TPU v7x, 128 devices: a whole 4x4x4 slice. The times are simulated.
128 devices in a mesh: inner: 8 (over z, core), outer: 16 (over x, y).
Axes of the slice: x: 4, y: 4, z: 4, core: 2. Of those that a mesh axis runs over, the one named last changes fastest.
Arguments:
- inner_state: float32 [2, 32, 2048], P(None, 'inner', 'outer'), may hold values from -6 to 6
- outer_state: float32 [2, 1280, 8192], P(None, 'inner', 'outer'), may hold values from -6 to 6
- energies: float32 [32, 2048], P('inner', 'outer'), may hold values from -2 to 2
- dipole: float32 [32, 2048, 2048], P('inner', 'outer'), may hold values from -0.125 to 0.125
- surface: float32 [32, 40, 2048], P('inner', None, 'outer'), may hold values from -0.125 to 0.125
- thresholds: float32 [1280], P('inner'), may hold values from 0 to 2
- coupling_coef: float32 [32, 40, 40], P('inner'), may hold values from -1 to 1
- coupling_pattern: int32 [32, 40, 40], P('inner'), may hold values 0 or 1
- block_sizes: int32 [32], P('inner'), may hold values from 1 to 2048, 61440 in all
- field_strength: float32 [2], replicated, may hold values from 0.5 to 2
Outputs:
- inner_final: float32 [2, 32, 2048], P(None, 'inner', 'outer')
- outer_final: float32 [2, 1280, 8192], P(None, 'inner', 'outer')
All inputs are finite; a program needn't handle non-finite values. No bound on the sum of `coupling_pattern` or of `block_sizes` on one device may be relied on, other than what follows from the above.
Results may differ from a plain program's by a relative error of at most 0.0001.
Values sent between devices are 32-bit elements; how exact they have to be, the bound alone decides.
No kernel may reach another device: no remote copies, remote signals or barrier semaphores. Data moves between devices by JAX's collectives and lax.ppermute only.
A program may use at most 128 MiB of HBM per device.

v0:
```python
import functools
import jax
import jax.numpy as jnp
from jax import lax
from jax.sharding import Mesh
from jax.sharding import PartitionSpec as P

STEPS = 2
ORDER = 4
OUTER = ("outer_0", "outer_1")
kinetic_scale = 3.125
time_step = 0.1


def cut_along(shard, dim, length):
    dims = shard.shape
    tiles = shard.reshape(*dims[:dim], length, dims[dim] // length, *dims[dim + 1 :])
    return jnp.moveaxis(tiles, dim, 0)


def sum_at_owner(shard, axis, dim):
    tiles = cut_along(shard, dim, lax.axis_size(axis))
    arrived = lax.all_to_all(tiles, axis, split_axis=0, concat_axis=0, tiled=True)
    return arrived.sum(axis=0)


def one_axis_at_a_time(shard, axes):
    return functools.reduce(lax.psum, axes, shard)


def from_behind(block, axis, distance):
    devices = range(lax.axis_size(axis))
    route = [(i - distance, i) for i in devices if i - distance in devices]
    return lax.ppermute(block, axis, route)


def laid_out(tiles, dim):
    tiles = jnp.moveaxis(tiles, 0, dim)
    dims = tiles.shape
    return tiles.reshape(*dims[:dim], dims[dim] * dims[dim + 1], *dims[dim + 2 :])


def from_everyone(shard, axis):
    copies = jnp.broadcast_to(shard, (lax.axis_size(axis), *shard.shape))
    return lax.all_to_all(copies, axis, split_axis=0, concat_axis=0, tiled=True)


def gathered_copies(shard, axis, dim):
    return laid_out(from_everyone(shard, axis), dim)


def broadcast_by_axis(shard, axes, root):
    shard = jnp.where(lax.axis_index(axes) == root, shard, jnp.zeros_like(shard))
    for axis in axes:
        shard = lax.psum(shard, axis)
    return shard


def with_halo(cells, sides, width):
    for axis, dim in sides:
        count = lax.axis_size(axis)
        ends = count - 1
        head = lax.slice_in_dim(cells, 0, width, axis=dim)
        tail = lax.slice_in_dim(cells, cells.shape[dim] - width, cells.shape[dim], axis=dim)
        cells = jnp.concatenate(
            [
                lax.ppermute(tail, axis, [(i, (i + 1) % count) for i in range(ends)]),
                cells,
                lax.ppermute(head, axis, [((i + 1) % count, i) for i in range(ends)]),
            ],
            axis=dim,
        )
    return cells


def reduce_partials(partial_terms, partial_boundary):
    own_terms = sum_at_owner(partial_terms, OUTER, 2)
    boundary = one_axis_at_a_time(partial_boundary, OUTER)
    return (own_terms, boundary)


def local(
    inner_state,
    outer_state,
    energies,
    dipole,
    surface,
    thresholds,
    coupling_coef,
    coupling_pattern,
    block_sizes,
    field_strength,
):
    highest = lax.Precision.HIGHEST
    blocks = dipole.shape[0]
    row_count = dipole.shape[1]
    channels = coupling_coef.shape[1]
    radial = outer_state.shape[2]
    sector_index = lax.axis_index(OUTER)
    row_index = sector_index * row_count + jnp.arange(row_count, dtype=jnp.int32)
    live_rows = (row_index[None, :] < block_sizes[:, None]).astype(jnp.float32)
    coupling = coupling_coef * coupling_pattern.astype(jnp.float32)
    first_sector = jnp.where(sector_index == 0, 1.0, 0.0).astype(jnp.float32)
    edge_mask = first_sector * (jnp.arange(radial, dtype=jnp.int32) == 0).astype(jnp.float32)
    current = (inner_state * live_rows, outer_state)
    for time_index in range(STEPS):
        strength = field_strength[time_index]
        taylor_term = current
        accumulated = current
        for power in range(1, ORDER + 1):
            inner_part = taylor_term[0]
            outer_part = taylor_term[1]
            channel_grid = outer_part.reshape(2, blocks, channels, radial)
            next_first, next_channels = from_behind(
                (inner_part[:, 0], channel_grid[:, 0]), "inner", -1
            )
            extended = jnp.concatenate([inner_part, next_first[:, None]], axis=1)
            gathered = gathered_copies(extended, OUTER, 2)
            edge_values = broadcast_by_axis(outer_part[:, :, 0], OUTER, 0)
            forward = jnp.einsum("lij,plj->pli", dipole, gathered[:, 1:], precision=highest)
            grid_next = jnp.concatenate([channel_grid[:, 1:], next_channels[:, None]], axis=1)
            upward = jnp.einsum("lab,plbr->plar", coupling, grid_next, precision=highest)
            partial_boundary = jnp.einsum("lcs,pls->plc", surface, inner_part, precision=highest)
            partial_terms = jnp.einsum("lji,plj->pli", dipole, inner_part, precision=highest)
            summed_terms, boundary = reduce_partials(partial_terms, partial_boundary)
            lowered = jnp.einsum("lba,plbr->plar", coupling, channel_grid, precision=highest)
            carried, carried_grid = from_behind(
                (summed_terms[:, blocks - 1], lowered[:, blocks - 1]), "inner", 1
            )
            backward = jnp.concatenate([carried[:, None], summed_terms[:, : blocks - 1]], axis=1)
            downward = jnp.concatenate([carried_grid[:, None], lowered[:, : blocks - 1]], axis=1)
            first_point = edge_values.reshape(2, blocks, channels)
            surf_term = jnp.einsum("lcs,plc->pls", surface, first_point, precision=highest)
            inner_image = live_rows * (
                energies * inner_part + strength * (forward + backward) - kinetic_scale * surf_term
            )
            padded = with_halo(outer_part, ((OUTER, 2),), 1)
            left_cells = (
                padded[:, :, :radial]
                + edge_mask[None, None, :] * boundary.reshape(2, blocks * channels)[:, :, None]
            )
            right_cells = padded[:, :, 2:]
            kinetic = kinetic_scale * (2.0 * outer_part - left_cells - right_cells)
            outer_image = (
                kinetic
                + thresholds[None, :, None] * outer_part
                + strength * (upward + downward).reshape(2, blocks * channels, radial)
            )
            inner_image, outer_image = (inner_image, outer_image)
            factor = time_step / power
            taylor_term = (
                factor * jnp.stack([inner_image[1], -inner_image[0]]),
                factor * jnp.stack([outer_image[1], -outer_image[0]]),
            )
            accumulated = (accumulated[0] + taylor_term[0], accumulated[1] + taylor_term[1])
        current = accumulated
    return (current[0], current[1])


def solution(mesh):
    torus = Mesh(mesh.devices.reshape(mesh.shape["inner"], 4, 4), ("inner", "outer_0", "outer_1"))
    placed = (
        P(None, "inner", OUTER),
        P(None, "inner", OUTER),
        P("inner", OUTER),
        P("inner", OUTER, None),
        P("inner", None, OUTER),
        P("inner"),
        P("inner", None, None),
        P("inner", None, None),
        P("inner"),
        P(),
    )
    return jax.shard_map(
        local,
        mesh=torus,
        in_specs=placed,
        out_specs=(P(None, "inner", OUTER), P(None, "inner", OUTER)),
        check_vma=False,
    )
```

profile of v0, /device:TPU:88, one launch (start us, length us, event | category | flops | bytes accessed | tf_op | source)
XLA Modules:
  0.0 597.7 jit_solution(16005529261771589149)
XLA Ops:
  9.2 7.2 %all-to-all-start.1 = ((f32[16,2,4,128]{3,1,2,0:T(2,128)}), f32[16,2,4,128]{3,1,2,0:T(2,128)S(1)}, u32[]{:S(2)}, u32[]{:S(2)}) async-start(f32[16,2,4,128]{3,1,2,0:T(2,128)} %bitcast.496), calls=%async_computation.1 | async-start | bytes 131072 | tf_op jit(solution)/shard_map/all_to_all | solution.py:23
  29.9 10.5 %all-reduce.15 = (f32[2,4,40]{2,0,1:T(2,128)S(1)}, f32[2,160]{1,0:T(2,128)S(1)}) all-reduce(f32[2,4,40]{2,0,1:T(2,128)S(1)} %convolution_bitcast_fusion.39, f32[2,160]{1,0:T(2,128)S(1)} %get-tuple-element.77), channel_id=1, replica_groups=mesh['inner'=8,'outer_0'=4,'outer_1'=4] {'outer_0'}, use_global_device_ids=true, to_apply=%region_4.5 | all-reduce | flops 640 | bytes 5120 | tf_op jit(solution)/shard_map/psum | solution.py:28
  40.6 9.3 %all-reduce.7 = (f32[2,160]{1,0:T(2,128)S(1)}, f32[2,4,40]{2,0,1:T(2,128)S(1)}) all-reduce(f32[2,160]{1,0:T(2,128)S(1)} %mul.604, f32[2,4,40]{2,0,1:T(2,128)S(1)} %copy.65), channel_id=1, replica_groups=mesh['inner'=8,'outer_0'=4,'outer_1'=4] {'outer_1'}, use_global_device_ids=true, to_apply=%region_5.6 | all-reduce | flops 640 | bytes 5120 | tf_op jit(solution)/shard_map/psum | solution.py:28
  50.6 5.1 all-to-all-start
  61.5 5.4 convolution_bitcast_fusion.31
  72.9 5.4 all-to-all-start.3
  78.3 5.8 all-to-all-done.3
  84.7 5.3 all-to-all-start.2
  95.8 5.2 convolution_bitcast_fusion.30
  105.0 8.8 %all-reduce.14 = (f32[2,4,40]{2,0,1:T(2,128)S(1)}, f32[2,160]{1,0:T(2,128)S(1)}) all-reduce(f32[2,4,40]{2,0,1:T(2,128)S(1)} %convolution_bitcast_fusion.38, f32[2,160]{1,0:T(2,128)S(1)} %get-tuple-element.72), channel_id=1, replica_groups=mesh['inner'=8,'outer_0'=4,'outer_1'=4] {'outer_0'}, use_global_device_ids=true, to_apply=%region_9.10 | all-reduce | flops 640 | bytes 5120 | tf_op jit(solution)/shard_map/psum | solution.py:28
  114.0 9.2 %all-reduce.6 = (f32[2,160]{1,0:T(2,128)}, f32[2,4,40]{2,0,1:T(2,128)S(1)}) all-reduce(f32[2,160]{1,0:T(2,128)S(1)} %mul.626, f32[2,4,40]{2,0,1:T(2,128)S(1)} %copy.74), channel_id=1, replica_groups=mesh['inner'=8,'outer_0'=4,'outer_1'=4] {'outer_1'}, use_global_device_ids=true, to_apply=%region_10.11 | all-reduce | flops 640 | bytes 5120 | tf_op jit(solution)/shard_map/psum | solution.py:28
  124.0 4.3 convolution_bitcast_fusion.21
  138.9 5.7 all-to-all-start.5
  151.1 7.3 %all-to-all-start.4 = ((f32[16,2,5,128]{3,1,2,0:T(2,128)}), f32[16,2,5,128]{3,1,2,0:T(2,128)S(1)}, u32[]{:S(2)}, u32[]{:S(2)}) async-start(f32[16,2,5,128]{3,1,2,0:T(2,128)} %broadcast_in_dim.164), calls=%async_computation.4 | async-start | bytes 163840 | tf_op jit(solution)/shard_map/all_to_all | solution.py:45
  164.3 5.2 convolution_bitcast_fusion.29
  176.1 8.9 %all-reduce.13 = (f32[2,4,40]{2,0,1:T(2,128)S(1)}, f32[2,160]{1,0:T(2,128)S(1)}) all-reduce(f32[2,4,40]{2,0,1:T(2,128)S(1)} %convolution_bitcast_fusion.37, f32[2,160]{1,0:T(2,128)S(1)} %get-tuple-element.67), channel_id=1, replica_groups=mesh['inner'=8,'outer_0'=4,'outer_1'=4] {'outer_0'}, use_global_device_ids=true, to_apply=%region_14.15 | all-reduce | flops 640 | bytes 5120 | tf_op jit(solution)/shard_map/psum | solution.py:28
  185.2 9.6 %all-reduce.5 = (f32[2,160]{1,0:T(2,128)}, f32[2,4,40]{2,0,1:T(2,128)S(1)}) all-reduce(f32[2,160]{1,0:T(2,128)S(1)} %mul.648, f32[2,4,40]{2,0,1:T(2,128)S(1)} %copy.80), channel_id=1, replica_groups=mesh['inner'=8,'outer_0'=4,'outer_1'=4] {'outer_1'}, use_global_device_ids=true, to_apply=%region_15.16 | all-reduce | flops 640 | bytes 5120 | tf_op jit(solution)/shard_map/psum | solution.py:28
  195.7 4.3 convolution_bitcast_fusion.20
  210.4 5.7 all-to-all-start.7
  223.9 7.4 %all-to-all-start.6 = ((f32[16,2,5,128]{3,1,2,0:T(2,128)}), f32[16,2,5,128]{3,1,2,0:T(2,128)S(1)}, u32[]{:S(2)}, u32[]{:S(2)}) async-start(f32[16,2,5,128]{3,1,2,0:T(2,128)} %broadcast_in_dim.169), calls=%async_computation.6 | async-start | bytes 163840 | tf_op jit(solution)/shard_map/all_to_all | solution.py:45
  237.1 5.3 convolution_bitcast_fusion.28
  249.8 8.9 %all-reduce.12 = (f32[2,4,40]{2,0,1:T(2,128)S(1)}, f32[2,160]{1,0:T(2,128)S(1)}) all-reduce(f32[2,4,40]{2,0,1:T(2,128)S(1)} %copy-done.81, f32[2,160]{1,0:T(2,128)S(1)} %get-tuple-element.62), channel_id=1, replica_groups=mesh['inner'=8,'outer_0'=4,'outer_1'=4] {'outer_0'}, use_global_device_ids=true, to_apply=%region_19.20 | all-reduce | flops 640 | bytes 5120 | tf_op jit(solution)/shard_map/psum | solution.py:28
  258.9 9.2 %all-reduce.4 = (f32[2,160]{1,0:T(2,128)}, f32[2,4,40]{2,0,1:T(2,128)S(1)}) all-reduce(f32[2,160]{1,0:T(2,128)S(1)} %mul.669, f32[2,4,40]{2,0,1:T(2,128)S(1)} %copy.86), channel_id=1, replica_groups=mesh['inner'=8,'outer_0'=4,'outer_1'=4] {'outer_1'}, use_global_device_ids=true, to_apply=%region_20.21 | all-reduce | flops 640 | bytes 5120 | tf_op jit(solution)/shard_map/psum | solution.py:28
  283.6 5.7 all-to-all-start.9
  297.1 7.4 %all-to-all-start.8 = ((f32[16,2,5,128]{3,1,2,0:T(2,128)}), f32[16,2,5,128]{3,1,2,0:T(2,128)S(1)}, u32[]{:S(2)}, u32[]{:S(2)}) async-start(f32[16,2,5,128]{3,1,2,0:T(2,128)} %broadcast_in_dim.174), calls=%async_computation.8 | async-start | bytes 163840 | tf_op jit(solution)/shard_map/all_to_all | solution.py:45
  310.3 5.9 convolution_bitcast_fusion.27
  322.2 9.5 %all-reduce.11 = (f32[2,4,40]{2,0,1:T(2,128)S(1)}, f32[2,160]{1,0:T(2,128)S(1)}) all-reduce(f32[2,4,40]{2,0,1:T(2,128)S(1)} %copy-done.82, f32[2,160]{1,0:T(2,128)S(1)} %get-tuple-element.57), channel_id=1, replica_groups=mesh['inner'=8,'outer_0'=4,'outer_1'=4] {'outer_0'}, use_global_device_ids=true, to_apply=%region_24.25 | all-reduce | flops 640 | bytes 5120 | tf_op jit(solution)/shard_map/psum | solution.py:28
  331.9 8.6 %all-reduce.3 = (f32[2,160]{1,0:T(2,128)}, f32[2,4,40]{2,0,1:T(2,128)S(1)}) all-reduce(f32[2,160]{1,0:T(2,128)S(1)} %mul.688, f32[2,4,40]{2,0,1:T(2,128)S(1)} %copy.92), channel_id=1, replica_groups=mesh['inner'=8,'outer_0'=4,'outer_1'=4] {'outer_1'}, use_global_device_ids=true, to_apply=%region_25.26 | all-reduce | flops 640 | bytes 5120 | tf_op jit(solution)/shard_map/psum | solution.py:28
  342.0 4.3 convolution_bitcast_fusion.18
  354.7 6.3 %all-to-all-start.11 = ((f32[16,2,4,128]{3,1,2,0:T(2,128)}), f32[16,2,4,128]{3,1,2,0:T(2,128)S(1)}, u32[]{:S(2)}, u32[]{:S(2)}) async-start(f32[16,2,4,128]{3,1,2,0:T(2,128)} %bitcast.527), calls=%async_computation.11 | async-start | bytes 131072 | tf_op jit(solution)/shard_map/all_to_all | solution.py:23
  372.6 7.4 %all-to-all-start.10 = ((f32[16,2,5,128]{3,1,2,0:T(2,128)}), f32[16,2,5,128]{3,1,2,0:T(2,128)S(1)}, u32[]{:S(2)}, u32[]{:S(2)}) async-start(f32[16,2,5,128]{3,1,2,0:T(2,128)} %broadcast_in_dim.179), calls=%async_computation.10 | async-start | bytes 163840 | tf_op jit(solution)/shard_map/all_to_all | solution.py:45
  386.1 5.9 convolution_bitcast_fusion.26
  400.3 10.7 %all-reduce.10 = (f32[2,4,40]{2,0,1:T(2,128)S(1)}, f32[2,160]{1,0:T(2,128)S(1)}) all-reduce(f32[2,4,40]{2,0,1:T(2,128)S(1)} %copy-done.79, f32[2,160]{1,0:T(2,128)S(1)} %get-tuple-element.52), channel_id=1, replica_groups=mesh['inner'=8,'outer_0'=4,'outer_1'=4] {'outer_0'}, use_global_device_ids=true, to_apply=%region_29.30 | all-reduce | flops 640 | bytes 5120 | tf_op jit(solution)/shard_map/psum | solution.py:28
  411.1 8.1 %all-reduce.2 = (f32[2,160]{1,0:T(2,128)}, f32[2,4,40]{2,0,1:T(2,128)S(1)}) all-reduce(f32[2,160]{1,0:T(2,128)S(1)} %mul.704, f32[2,4,40]{2,0,1:T(2,128)S(1)} %copy.101), channel_id=1, replica_groups=mesh['inner'=8,'outer_0'=4,'outer_1'=4] {'outer_1'}, use_global_device_ids=true, to_apply=%region_30.31 | all-reduce | flops 640 | bytes 5120 | tf_op jit(solution)/shard_map/psum | solution.py:28
  421.0 4.3 convolution_bitcast_fusion.17
  435.6 6.8 %all-to-all-start.13 = ((f32[16,2,4,128]{3,1,2,0:T(2,128)}), f32[16,2,4,128]{3,1,2,0:T(2,128)S(1)}, u32[]{:S(2)}, u32[]{:S(2)}) async-start(f32[16,2,4,128]{3,1,2,0:T(2,128)} %bitcast.528), calls=%async_computation.13 | async-start | bytes 131072 | tf_op jit(solution)/shard_map/all_to_all | solution.py:23
  450.1 7.4 %all-to-all-start.12 = ((f32[16,2,5,128]{3,1,2,0:T(2,128)}), f32[16,2,5,128]{3,1,2,0:T(2,128)S(1)}, u32[]{:S(2)}, u32[]{:S(2)}) async-start(f32[16,2,5,128]{3,1,2,0:T(2,128)} %broadcast_in_dim.184), calls=%async_computation.12 | async-start | bytes 163840 | tf_op jit(solution)/shard_map/all_to_all | solution.py:45
  463.3 6.0 convolution_bitcast_fusion.25
  477.0 9.3 %all-reduce.9 = (f32[2,4,40]{2,0,1:T(2,128)S(1)}, f32[2,160]{1,0:T(2,128)S(1)}) all-reduce(f32[2,4,40]{2,0,1:T(2,128)S(1)} %copy-done.80, f32[2,160]{1,0:T(2,128)S(1)} %get-tuple-element.47), channel_id=1, replica_groups=mesh['inner'=8,'outer_0'=4,'outer_1'=4] {'outer_0'}, use_global_device_ids=true, to_apply=%region_34.35 | all-reduce | flops 640 | bytes 5120 | tf_op jit(solution)/shard_map/psum | solution.py:28
  486.5 8.7 %all-reduce.1 = (f32[2,160]{1,0:T(2,128)}, f32[2,4,40]{2,0,1:T(2,128)S(1)}) all-reduce(f32[2,160]{1,0:T(2,128)S(1)} %mul.720, f32[2,4,40]{2,0,1:T(2,128)S(1)} %copy.107), channel_id=1, replica_groups=mesh['inner'=8,'outer_0'=4,'outer_1'=4] {'outer_1'}, use_global_device_ids=true, to_apply=%region_35.36 | all-reduce | flops 640 | bytes 5120 | tf_op jit(solution)/shard_map/psum | solution.py:28
  496.9 4.3 convolution_bitcast_fusion.16
  511.5 6.2 %all-to-all-start.15 = ((f32[16,2,4,128]{3,1,2,0:T(2,128)}), f32[16,2,4,128]{3,1,2,0:T(2,128)S(1)}, u32[]{:S(2)}, u32[]{:S(2)}) async-start(f32[16,2,4,128]{3,1,2,0:T(2,128)} %bitcast.529), calls=%async_computation.15 | async-start | bytes 131072 | tf_op jit(solution)/shard_map/all_to_all | solution.py:23
  525.4 7.4 %all-to-all-start.14 = ((f32[16,2,5,128]{3,1,2,0:T(2,128)}), f32[16,2,5,128]{3,1,2,0:T(2,128)S(1)}, u32[]{:S(2)}, u32[]{:S(2)}) async-start(f32[16,2,5,128]{3,1,2,0:T(2,128)} %broadcast_in_dim.189), calls=%async_computation.14 | async-start | bytes 163840 | tf_op jit(solution)/shard_map/all_to_all | solution.py:45
  538.6 6.0 %convolution_bitcast_fusion.24 = f32[2,4,128]{2,0,1:T(2,128)} fusion(f32[4,128,2048]{2,1,0:T(8,128)} %param.13, f32[16,2,5,128]{3,1,2,0:T(2,128)S(1)} %all-to-all-done.14), kind=kOutput, calls=%fused_computation.40 | convolution fusion | flops 25165824 | bytes 4280320 | tf_op jit(solution)/shard_map/lij,plj->pli/dot_general | solution.py:120
  559.2 9.6 %all-reduce.8 = (f32[2,160]{1,0:T(2,128)S(1)}, f32[2,4,40]{2,0,1:T(2,128)S(1)}) all-reduce(f32[2,160]{1,0:T(2,128)S(1)} %get-tuple-element.43, f32[2,4,40]{2,0,1:T(2,128)S(1)} %copy-done.78), channel_id=1, replica_groups=mesh['inner'=8,'outer_0'=4,'outer_1'=4] {'outer_0'}, use_global_device_ids=true, to_apply=%region_36.37 | all-reduce | flops 640 | bytes 5120 | tf_op jit(solution)/shard_map/psum | solution.py:55
  569.0 7.9 %all-reduce = (f32[2,4,40]{2,0,1:T(2,128)S(1)}, f32[2,160]{1,0:T(2,128)S(1)}) all-reduce(f32[2,4,40]{2,0,1:T(2,128)S(1)} %copy.113, f32[2,160]{1,0:T(2,128)S(1)} %mul.734), channel_id=1, replica_groups=mesh['inner'=8,'outer_0'=4,'outer_1'=4] {'outer_1'}, use_global_device_ids=true, to_apply=%region_37.38 | all-reduce | flops 640 | bytes 5120 | tf_op jit(solution)/shard_map/psum | solution.py:55
  579.3 4.7 collective-permute-start.44
  588.7 4.9 collective-permute-done.45
  (544 shorter events, 261.9 us)
Async XLA Ops:
  2.2 47.7 %collective-permute-start = (f32[2,128]{1,0:T(2,128)S(1)}, f32[2,128]{1,0:T(2,128)S(1)}, u32[]{:S(2)}, u32[]{:S(2)}) collective-permute-start(f32[2,128]{1,0:T(2,128)S(1)} %slice_bitcast_fusion.31), channel_id=1, source_target_pairs={{16,0},{32,16},{48,32},{64,48},{80,64},{96,80},{112,96},{17,1},{33... | collective-permute-start | bytes 3080 | tf_op jit(solution)/shard_map/ppermute | solution.py:34
  9.2 40.7 %all-to-all-start.1 = ((f32[16,2,4,128]{3,1,2,0:T(2,128)}), f32[16,2,4,128]{3,1,2,0:T(2,128)S(1)}, u32[]{:S(2)}, u32[]{:S(2)}) async-start(f32[16,2,4,128]{3,1,2,0:T(2,128)} %bitcast.496), calls=%async_computation.1 | async-start | bytes 131072 | tf_op jit(solution)/shard_map/all_to_all | solution.py:23
  16.4 84.7 %collective-permute-start.6 = (f32[2,40,512]{2,1,0:T(8,128)S(1)}, f32[2,40,512]{2,1,0:T(8,128)S(1)}, u32[]{:S(2)}, u32[]{:S(2)}) collective-permute-start(f32[2,40,512]{2,1,0:T(8,128)S(1)} %slice_bitcast_fusion.15), channel_id=1, source_target_pairs={{16,0},{32,16},{48,32},{64,48},{80,64},{96,80},{112,96},{17,1},{33... | collective-permute-start | bytes 491528 | tf_op jit(solution)/shard_map/ppermute | solution.py:34
  19.1 83.4 %collective-permute-start.4 = (f32[2,160,1]{2,1,0:T(8,128)}, f32[2,160,1]{2,1,0:T(8,128)S(1)}, u32[]{:S(2)}, u32[]{:S(2)}) collective-permute-start(f32[2,160,1]{2,1,0:T(8,128)} %get-tuple-element.78), channel_id=1, source_target_pairs={{0,1},{1,2},{2,3},{3,4},{4,5},{5,6},{6,7},{7,8},{8,9},{9,10},{10,1... | collective-permute-start | bytes 3848 | tf_op jit(solution)/shard_map/ppermute | solution.py:67
  22.4 80.1 %collective-permute-start.5 = (f32[2,160,1]{2,1,0:T(8,128)}, f32[2,160,1]{2,1,0:T(8,128)S(1)}, u32[]{:S(2)}, u32[]{:S(2)}) collective-permute-start(f32[2,160,1]{2,1,0:T(8,128)} %get-tuple-element.79), channel_id=1, source_target_pairs={{1,0},{2,1},{3,2},{4,3},{5,4},{6,5},{7,6},{8,7},{9,8},{10,9},{11,1... | collective-permute-start | bytes 3848 | tf_op jit(solution)/shard_map/ppermute | solution.py:69
  26.4 74.7 %collective-permute-start.7 = (f32[2,40,512]{2,1,0:T(8,128)}, f32[2,40,512]{2,1,0:T(8,128)S(1)}, u32[]{:S(2)}, u32[]{:S(2)}) collective-permute-start(f32[2,40,512]{2,1,0:T(8,128)} %slice_bitcast_fusion.14), channel_id=1, source_target_pairs={{0,16},{16,32},{32,48},{48,64},{64,80},{80,96},{96,112},{1,17},{17... | collective-permute-start | bytes 491528 | tf_op jit(solution)/shard_map/ppermute | solution.py:34
  90.0 33.2 %collective-permute-start.3 = (f32[2,128]{1,0:T(2,128)S(1)}, f32[2,128]{1,0:T(2,128)S(1)}, u32[]{:S(2)}, u32[]{:S(2)}) collective-permute-start(f32[2,128]{1,0:T(2,128)S(1)} %slice_bitcast_fusion.28), channel_id=1, source_target_pairs={{0,16},{16,32},{32,48},{48,64},{64,80},{80,96},{96,112},{1,17},{17... | collective-permute-start | bytes 3080 | tf_op jit(solution)/shard_map/ppermute | solution.py:34
  130.2 20.2 %collective-permute-start.8 = (f32[2,128]{1,0:T(2,128)}, f32[2,128]{1,0:T(2,128)S(1)}, u32[]{:S(2)}, u32[]{:S(2)}) collective-permute-start(f32[2,128]{1,0:T(2,128)} %slice_bitcast_fusion.27), channel_id=1, source_target_pairs={{16,0},{32,16},{48,32},{64,48},{80,64},{96,80},{112,96},{17,1},{33... | collective-permute-start | bytes 3080 | tf_op jit(solution)/shard_map/ppermute | solution.py:34
  132.4 37.2 %collective-permute-start.13 = (f32[2,40,512]{2,1,0:T(8,128)}, f32[2,40,512]{2,1,0:T(8,128)S(1)}, u32[]{:S(2)}, u32[]{:S(2)}) collective-permute-start(f32[2,40,512]{2,1,0:T(8,128)} %slice_bitcast_fusion.12), channel_id=1, source_target_pairs={{0,16},{16,32},{32,48},{48,64},{64,80},{80,96},{96,112},{1,17},{17... | collective-permute-start | bytes 491528 | tf_op jit(solution)/shard_map/ppermute | solution.py:34
  134.9 34.6 %collective-permute-start.12 = (f32[2,40,512]{2,1,0:T(8,128)}, f32[2,40,512]{2,1,0:T(8,128)}, u32[]{:S(2)}, u32[]{:S(2)}) collective-permute-start(f32[2,40,512]{2,1,0:T(8,128)} %slice_bitcast_fusion.13), channel_id=1, source_target_pairs={{16,0},{32,16},{48,32},{64,48},{80,64},{96,80},{112,96},{17,1},{33... | collective-permute-start | bytes 491528 | tf_op jit(solution)/shard_map/ppermute | solution.py:34
  144.6 27.3 %collective-permute-start.10 = (f32[2,160,1]{2,1,0:T(8,128)}, f32[2,160,1]{2,1,0:T(8,128)}, u32[]{:S(2)}, u32[]{:S(2)}) collective-permute-start(f32[2,160,1]{2,1,0:T(8,128)} %get-tuple-element.73), channel_id=1, source_target_pairs={{0,1},{1,2},{2,3},{3,4},{4,5},{5,6},{6,7},{7,8},{8,9},{9,10},{10,1... | collective-permute-start | bytes 3848 | tf_op jit(solution)/shard_map/ppermute | solution.py:67
  148.0 23.9 %collective-permute-start.11 = (f32[2,160,1]{2,1,0:T(8,128)}, f32[2,160,1]{2,1,0:T(8,128)}, u32[]{:S(2)}, u32[]{:S(2)}) collective-permute-start(f32[2,160,1]{2,1,0:T(8,128)} %get-tuple-element.74), channel_id=1, source_target_pairs={{1,0},{2,1},{3,2},{4,3},{5,4},{6,5},{7,6},{8,7},{9,8},{10,9},{11,1... | collective-permute-start | bytes 3848 | tf_op jit(solution)/shard_map/ppermute | solution.py:69
  158.5 36.2 %collective-permute-start.9 = (f32[2,128]{1,0:T(2,128)S(1)}, f32[2,128]{1,0:T(2,128)S(1)}, u32[]{:S(2)}, u32[]{:S(2)}) collective-permute-start(f32[2,128]{1,0:T(2,128)S(1)} %slice_bitcast_fusion.26), channel_id=1, source_target_pairs={{0,16},{16,32},{32,48},{48,64},{64,80},{80,96},{96,112},{1,17},{17... | collective-permute-start | bytes 3080 | tf_op jit(solution)/shard_map/ppermute | solution.py:34
  201.3 20.7 %collective-permute-start.14 = (f32[2,128]{1,0:T(2,128)S(1)}, f32[2,128]{1,0:T(2,128)S(1)}, u32[]{:S(2)}, u32[]{:S(2)}) collective-permute-start(f32[2,128]{1,0:T(2,128)S(1)} %slice_bitcast_fusion.25), channel_id=1, source_target_pairs={{16,0},{32,16},{48,32},{64,48},{80,64},{96,80},{112,96},{17,1},{33... | collective-permute-start | bytes 3080 | tf_op jit(solution)/shard_map/ppermute | solution.py:34
  204.0 38.4 %collective-permute-start.19 = (f32[2,40,512]{2,1,0:T(8,128)}, f32[2,40,512]{2,1,0:T(8,128)}, u32[]{:S(2)}, u32[]{:S(2)}) collective-permute-start(f32[2,40,512]{2,1,0:T(8,128)} %slice_bitcast_fusion.10), channel_id=1, source_target_pairs={{0,16},{16,32},{32,48},{48,64},{64,80},{80,96},{96,112},{1,17},{17... | collective-permute-start | bytes 491528 | tf_op jit(solution)/shard_map/ppermute | solution.py:34
  206.5 35.9 %collective-permute-start.18 = (f32[2,40,512]{2,1,0:T(8,128)}, f32[2,40,512]{2,1,0:T(8,128)}, u32[]{:S(2)}, u32[]{:S(2)}) collective-permute-start(f32[2,40,512]{2,1,0:T(8,128)} %slice_bitcast_fusion.11), channel_id=1, source_target_pairs={{16,0},{32,16},{48,32},{64,48},{80,64},{96,80},{112,96},{17,1},{33... | collective-permute-start | bytes 491528 | tf_op jit(solution)/shard_map/ppermute | solution.py:34
  216.1 28.7 %collective-permute-start.16 = (f32[2,160,1]{2,1,0:T(8,128)}, f32[2,160,1]{2,1,0:T(8,128)}, u32[]{:S(2)}, u32[]{:S(2)}) collective-permute-start(f32[2,160,1]{2,1,0:T(8,128)} %get-tuple-element.68), channel_id=1, source_target_pairs={{0,1},{1,2},{2,3},{3,4},{4,5},{5,6},{6,7},{7,8},{8,9},{9,10},{10,1... | collective-permute-start | bytes 3848 | tf_op jit(solution)/shard_map/ppermute | solution.py:67
  219.5 25.3 %collective-permute-start.17 = (f32[2,160,1]{2,1,0:T(8,128)}, f32[2,160,1]{2,1,0:T(8,128)}, u32[]{:S(2)}, u32[]{:S(2)}) collective-permute-start(f32[2,160,1]{2,1,0:T(8,128)} %get-tuple-element.69), channel_id=1, source_target_pairs={{1,0},{2,1},{3,2},{4,3},{5,4},{6,5},{7,6},{8,7},{9,8},{10,9},{11,1... | collective-permute-start | bytes 3848 | tf_op jit(solution)/shard_map/ppermute | solution.py:69
  231.3 36.7 %collective-permute-start.15 = (f32[2,128]{1,0:T(2,128)S(1)}, f32[2,128]{1,0:T(2,128)S(1)}, u32[]{:S(2)}, u32[]{:S(2)}) collective-permute-start(f32[2,128]{1,0:T(2,128)S(1)} %slice_bitcast_fusion.24), channel_id=1, source_target_pairs={{0,16},{16,32},{32,48},{48,64},{64,80},{80,96},{96,112},{1,17},{17... | collective-permute-start | bytes 3080 | tf_op jit(solution)/shard_map/ppermute | solution.py:34
  274.7 20.6 %collective-permute-start.20 = (f32[2,128]{1,0:T(2,128)S(1)}, f32[2,128]{1,0:T(2,128)S(1)}, u32[]{:S(2)}, u32[]{:S(2)}) collective-permute-start(f32[2,128]{1,0:T(2,128)S(1)} %slice_bitcast_fusion.23), channel_id=1, source_target_pairs={{16,0},{32,16},{48,32},{64,48},{80,64},{96,80},{112,96},{17,1},{33... | collective-permute-start | bytes 3080 | tf_op jit(solution)/shard_map/ppermute | solution.py:34
  277.4 38.8 %collective-permute-start.25 = (f32[2,40,512]{2,1,0:T(8,128)}, f32[2,40,512]{2,1,0:T(8,128)}, u32[]{:S(2)}, u32[]{:S(2)}) collective-permute-start(f32[2,40,512]{2,1,0:T(8,128)} %slice_bitcast_fusion.8), channel_id=1, source_target_pairs={{0,16},{16,32},{32,48},{48,64},{64,80},{80,96},{96,112},{1,17},{17... | collective-permute-start | bytes 491528 | tf_op jit(solution)/shard_map/ppermute | solution.py:34
  279.8 36.4 %collective-permute-start.24 = (f32[2,40,512]{2,1,0:T(8,128)}, f32[2,40,512]{2,1,0:T(8,128)}, u32[]{:S(2)}, u32[]{:S(2)}) collective-permute-start(f32[2,40,512]{2,1,0:T(8,128)} %slice_bitcast_fusion.9), channel_id=1, source_target_pairs={{16,0},{32,16},{48,32},{64,48},{80,64},{96,80},{112,96},{17,1},{33... | collective-permute-start | bytes 491528 | tf_op jit(solution)/shard_map/ppermute | solution.py:34
  289.4 29.3 %collective-permute-start.22 = (f32[2,160,1]{2,1,0:T(8,128)}, f32[2,160,1]{2,1,0:T(8,128)}, u32[]{:S(2)}, u32[]{:S(2)}) collective-permute-start(f32[2,160,1]{2,1,0:T(8,128)} %get-tuple-element.63), channel_id=1, source_target_pairs={{0,1},{1,2},{2,3},{3,4},{4,5},{5,6},{6,7},{7,8},{8,9},{9,10},{10,1... | collective-permute-start | bytes 3848 | tf_op jit(solution)/shard_map/ppermute | solution.py:67
  292.7 25.9 %collective-permute-start.23 = (f32[2,160,1]{2,1,0:T(8,128)}, f32[2,160,1]{2,1,0:T(8,128)}, u32[]{:S(2)}, u32[]{:S(2)}) collective-permute-start(f32[2,160,1]{2,1,0:T(8,128)} %get-tuple-element.64), channel_id=1, source_target_pairs={{1,0},{2,1},{3,2},{4,3},{5,4},{6,5},{7,6},{8,7},{9,8},{10,9},{11,1... | collective-permute-start | bytes 3848 | tf_op jit(solution)/shard_map/ppermute | solution.py:69
  307.2 33.3 %collective-permute-start.21 = (f32[2,128]{1,0:T(2,128)}, f32[2,128]{1,0:T(2,128)}, u32[]{:S(2)}, u32[]{:S(2)}) collective-permute-start(f32[2,128]{1,0:T(2,128)} %slice_bitcast_fusion.22), channel_id=1, source_target_pairs={{0,16},{16,32},{32,48},{48,64},{64,80},{80,96},{96,112},{1,17},{17... | collective-permute-start | bytes 3080 | tf_op jit(solution)/shard_map/ppermute | solution.py:34
  347.7 23.0 %collective-permute-start.26 = (f32[2,128]{1,0:T(2,128)S(1)}, f32[2,128]{1,0:T(2,128)S(1)}, u32[]{:S(2)}, u32[]{:S(2)}) collective-permute-start(f32[2,128]{1,0:T(2,128)S(1)} %slice_bitcast_fusion.21), channel_id=1, source_target_pairs={{16,0},{32,16},{48,32},{64,48},{80,64},{96,80},{112,96},{17,1},{33... | collective-permute-start | bytes 3080 | tf_op jit(solution)/shard_map/ppermute | solution.py:34
  351.9 40.1 %collective-permute-start.30 = (f32[2,40,512]{2,1,0:T(8,128)}, f32[2,40,512]{2,1,0:T(8,128)}, u32[]{:S(2)}, u32[]{:S(2)}) collective-permute-start(f32[2,40,512]{2,1,0:T(8,128)} %slice_bitcast_fusion.7), channel_id=1, source_target_pairs={{16,0},{32,16},{48,32},{64,48},{80,64},{96,80},{112,96},{17,1},{33... | collective-permute-start | bytes 491528 | tf_op jit(solution)/shard_map/ppermute | solution.py:34
  354.7 17.3 %all-to-all-start.11 = ((f32[16,2,4,128]{3,1,2,0:T(2,128)}), f32[16,2,4,128]{3,1,2,0:T(2,128)S(1)}, u32[]{:S(2)}, u32[]{:S(2)}) async-start(f32[16,2,4,128]{3,1,2,0:T(2,128)} %bitcast.527), calls=%async_computation.11 | async-start | bytes 131072 | tf_op jit(solution)/shard_map/all_to_all | solution.py:23
  361.0 33.5 %collective-permute-start.28 = (f32[2,160,1]{2,1,0:T(8,128)}, f32[2,160,1]{2,1,0:T(8,128)}, u32[]{:S(2)}, u32[]{:S(2)}) collective-permute-start(f32[2,160,1]{2,1,0:T(8,128)} %get-tuple-element.58), channel_id=1, source_target_pairs={{0,1},{1,2},{2,3},{3,4},{4,5},{5,6},{6,7},{7,8},{8,9},{9,10},{10,1... | collective-permute-start | bytes 3848 | tf_op jit(solution)/shard_map/ppermute | solution.py:67
  364.4 30.1 %collective-permute-start.29 = (f32[2,160,1]{2,1,0:T(8,128)}, f32[2,160,1]{2,1,0:T(8,128)}, u32[]{:S(2)}, u32[]{:S(2)}) collective-permute-start(f32[2,160,1]{2,1,0:T(8,128)} %get-tuple-element.59), channel_id=1, source_target_pairs={{1,0},{2,1},{3,2},{4,3},{5,4},{6,5},{7,6},{8,7},{9,8},{10,9},{11,1... | collective-permute-start | bytes 3848 | tf_op jit(solution)/shard_map/ppermute | solution.py:69
  368.7 23.3 %collective-permute-start.31 = (f32[2,40,512]{2,1,0:T(8,128)}, f32[2,40,512]{2,1,0:T(8,128)}, u32[]{:S(2)}, u32[]{:S(2)}) collective-permute-start(f32[2,40,512]{2,1,0:T(8,128)} %slice_bitcast_fusion.6), channel_id=1, source_target_pairs={{0,16},{16,32},{32,48},{48,64},{64,80},{80,96},{96,112},{1,17},{17... | collective-permute-start | bytes 491528 | tf_op jit(solution)/shard_map/ppermute | solution.py:34
  372.6 13.5 %all-to-all-start.10 = ((f32[16,2,5,128]{3,1,2,0:T(2,128)}), f32[16,2,5,128]{3,1,2,0:T(2,128)S(1)}, u32[]{:S(2)}, u32[]{:S(2)}) async-start(f32[16,2,5,128]{3,1,2,0:T(2,128)} %broadcast_in_dim.179), calls=%async_computation.10 | async-start | bytes 163840 | tf_op jit(solution)/shard_map/all_to_all | solution.py:45
  382.7 36.6 %collective-permute-start.27 = (f32[2,128]{1,0:T(2,128)}, f32[2,128]{1,0:T(2,128)}, u32[]{:S(2)}, u32[]{:S(2)}) collective-permute-start(f32[2,128]{1,0:T(2,128)} %slice_bitcast_fusion.20), channel_id=1, source_target_pairs={{0,16},{16,32},{32,48},{48,64},{64,80},{80,96},{96,112},{1,17},{17... | collective-permute-start | bytes 3080 | tf_op jit(solution)/shard_map/ppermute | solution.py:34
  426.6 21.6 %collective-permute-start.32 = (f32[2,128]{1,0:T(2,128)S(1)}, f32[2,128]{1,0:T(2,128)S(1)}, u32[]{:S(2)}, u32[]{:S(2)}) collective-permute-start(f32[2,128]{1,0:T(2,128)S(1)} %slice_bitcast_fusion.19), channel_id=1, source_target_pairs={{16,0},{32,16},{48,32},{64,48},{80,64},{96,80},{112,96},{17,1},{33... | collective-permute-start | bytes 3080 | tf_op jit(solution)/shard_map/ppermute | solution.py:34
  429.4 40.0 %collective-permute-start.37 = (f32[2,40,512]{2,1,0:T(8,128)}, f32[2,40,512]{2,1,0:T(8,128)}, u32[]{:S(2)}, u32[]{:S(2)}) collective-permute-start(f32[2,40,512]{2,1,0:T(8,128)} %slice_bitcast_fusion.4), channel_id=1, source_target_pairs={{0,16},{16,32},{32,48},{48,64},{64,80},{80,96},{96,112},{1,17},{17... | collective-permute-start | bytes 491528 | tf_op jit(solution)/shard_map/ppermute | solution.py:34
  431.8 37.6 %collective-permute-start.36 = (f32[2,40,512]{2,1,0:T(8,128)}, f32[2,40,512]{2,1,0:T(8,128)}, u32[]{:S(2)}, u32[]{:S(2)}) collective-permute-start(f32[2,40,512]{2,1,0:T(8,128)} %slice_bitcast_fusion.5), channel_id=1, source_target_pairs={{16,0},{32,16},{48,32},{64,48},{80,64},{96,80},{112,96},{17,1},{33... | collective-permute-start | bytes 491528 | tf_op jit(solution)/shard_map/ppermute | solution.py:34
  435.6 13.9 %all-to-all-start.13 = ((f32[16,2,4,128]{3,1,2,0:T(2,128)}), f32[16,2,4,128]{3,1,2,0:T(2,128)S(1)}, u32[]{:S(2)}, u32[]{:S(2)}) async-start(f32[16,2,4,128]{3,1,2,0:T(2,128)} %bitcast.528), calls=%async_computation.13 | async-start | bytes 131072 | tf_op jit(solution)/shard_map/all_to_all | solution.py:23
  442.4 29.4 %collective-permute-start.34 = (f32[2,160,1]{2,1,0:T(8,128)}, f32[2,160,1]{2,1,0:T(8,128)}, u32[]{:S(2)}, u32[]{:S(2)}) collective-permute-start(f32[2,160,1]{2,1,0:T(8,128)} %get-tuple-element.53), channel_id=1, source_target_pairs={{0,1},{1,2},{2,3},{3,4},{4,5},{5,6},{6,7},{7,8},{8,9},{9,10},{10,1... | collective-permute-start | bytes 3848 | tf_op jit(solution)/shard_map/ppermute | solution.py:67
  445.7 26.0 %collective-permute-start.35 = (f32[2,160,1]{2,1,0:T(8,128)}, f32[2,160,1]{2,1,0:T(8,128)}, u32[]{:S(2)}, u32[]{:S(2)}) collective-permute-start(f32[2,160,1]{2,1,0:T(8,128)} %get-tuple-element.54), channel_id=1, source_target_pairs={{1,0},{2,1},{3,2},{4,3},{5,4},{6,5},{7,6},{8,7},{9,8},{10,9},{11,1... | collective-permute-start | bytes 3848 | tf_op jit(solution)/shard_map/ppermute | solution.py:69
  460.2 35.0 %collective-permute-start.33 = (f32[2,128]{1,0:T(2,128)}, f32[2,128]{1,0:T(2,128)}, u32[]{:S(2)}, u32[]{:S(2)}) collective-permute-start(f32[2,128]{1,0:T(2,128)} %slice_bitcast_fusion.18), channel_id=1, source_target_pairs={{0,16},{16,32},{32,48},{48,64},{64,80},{80,96},{96,112},{1,17},{17... | collective-permute-start | bytes 3080 | tf_op jit(solution)/shard_map/ppermute | solution.py:34
  502.5 21.0 %collective-permute-start.38 = (f32[2,128]{1,0:T(2,128)S(1)}, f32[2,128]{1,0:T(2,128)S(1)}, u32[]{:S(2)}, u32[]{:S(2)}) collective-permute-start(f32[2,128]{1,0:T(2,128)S(1)} %slice_bitcast_fusion.17), channel_id=1, source_target_pairs={{16,0},{32,16},{48,32},{64,48},{80,64},{96,80},{112,96},{17,1},{33... | collective-permute-start | bytes 3080 | tf_op jit(solution)/shard_map/ppermute | solution.py:34
  505.2 39.4 %collective-permute-start.43 = (f32[2,40,512]{2,1,0:T(8,128)}, f32[2,40,512]{2,1,0:T(8,128)}, u32[]{:S(2)}, u32[]{:S(2)}) collective-permute-start(f32[2,40,512]{2,1,0:T(8,128)} %slice_bitcast_fusion.2), channel_id=1, source_target_pairs={{0,16},{16,32},{32,48},{48,64},{64,80},{80,96},{96,112},{1,17},{17... | collective-permute-start | bytes 491528 | tf_op jit(solution)/shard_map/ppermute | solution.py:34
  507.6 37.0 %collective-permute-start.42 = (f32[2,40,512]{2,1,0:T(8,128)}, f32[2,40,512]{2,1,0:T(8,128)}, u32[]{:S(2)}, u32[]{:S(2)}) collective-permute-start(f32[2,40,512]{2,1,0:T(8,128)} %slice_bitcast_fusion.3), channel_id=1, source_target_pairs={{16,0},{32,16},{48,32},{64,48},{80,64},{96,80},{112,96},{17,1},{33... | collective-permute-start | bytes 491528 | tf_op jit(solution)/shard_map/ppermute | solution.py:34
  517.7 29.4 %collective-permute-start.40 = (f32[2,160,1]{2,1,0:T(8,128)}, f32[2,160,1]{2,1,0:T(8,128)}, u32[]{:S(2)}, u32[]{:S(2)}) collective-permute-start(f32[2,160,1]{2,1,0:T(8,128)} %get-tuple-element.48), channel_id=1, source_target_pairs={{0,1},{1,2},{2,3},{3,4},{4,5},{5,6},{6,7},{7,8},{8,9},{9,10},{10,1... | collective-permute-start | bytes 3848 | tf_op jit(solution)/shard_map/ppermute | solution.py:67
  521.0 26.1 %collective-permute-start.41 = (f32[2,160,1]{2,1,0:T(8,128)}, f32[2,160,1]{2,1,0:T(8,128)}, u32[]{:S(2)}, u32[]{:S(2)}) collective-permute-start(f32[2,160,1]{2,1,0:T(8,128)} %get-tuple-element.49), channel_id=1, source_target_pairs={{1,0},{2,1},{3,2},{4,3},{5,4},{6,5},{7,6},{8,7},{9,8},{10,9},{11,1... | collective-permute-start | bytes 3848 | tf_op jit(solution)/shard_map/ppermute | solution.py:69
  535.5 41.4 %collective-permute-start.39 = (f32[2,128]{1,0:T(2,128)}, f32[2,128]{1,0:T(2,128)}, u32[]{:S(2)}, u32[]{:S(2)}) collective-permute-start(f32[2,128]{1,0:T(2,128)} %slice_bitcast_fusion.16), channel_id=1, source_target_pairs={{0,16},{16,32},{32,48},{48,64},{64,80},{80,96},{96,112},{1,17},{17... | collective-permute-start | bytes 3080 | tf_op jit(solution)/shard_map/ppermute | solution.py:34
  552.8 33.2 %collective-permute-start.47 = (f32[2,40,512]{2,1,0:T(8,128)}, f32[2,40,512]{2,1,0:T(8,128)}, u32[]{:S(2)}, u32[]{:S(2)}) collective-permute-start(f32[2,40,512]{2,1,0:T(8,128)} %slice_bitcast_fusion), channel_id=1, source_target_pairs={{0,16},{16,32},{32,48},{48,64},{64,80},{80,96},{96,112},{1,17},{17... | collective-permute-start | bytes 491528 | tf_op jit(solution)/shard_map/ppermute | solution.py:34
  554.7 31.2 %collective-permute-start.46 = (f32[2,40,512]{2,1,0:T(8,128)}, f32[2,40,512]{2,1,0:T(8,128)}, u32[]{:S(2)}, u32[]{:S(2)}) collective-permute-start(f32[2,40,512]{2,1,0:T(8,128)} %slice_bitcast_fusion.1), channel_id=1, source_target_pairs={{16,0},{32,16},{48,32},{64,48},{80,64},{96,80},{112,96},{17,1},{33... | collective-permute-start | bytes 491528 | tf_op jit(solution)/shard_map/ppermute | solution.py:34
  (129 other events, 2866.1 us)
where the time goes:
time: 608 us; the launch traced here: 598 us
  starting transfers between devices  226 us (37%)
  blocking collectives  147 us (24%)
  matrix products  118 us (19%)
  local copies, waits for them, and re-layouts  38.2 us (6%)
  other arithmetic  35.6 us (6%)
  waiting for transfers between devices  29.2 us (5%)
    psum x14, blocking collectives, one_axis_at_a_time(): return functools.reduce(lax.psum, axes, shard)  129 us
    ppermute x32, starting transfers between devices, from_behind(): return lax.ppermute(block, axis, route)  74.6 us
    all_to_all x8, starting transfers between devices, from_everyone(): return lax.all_to_all(copies, axis, split_axis=0, concat_axis=0, tiled=True)  54.6 us
    all_to_all x8, starting transfers between devices, sum_at_owner(): lax.all_to_all(tiles, axis, split_axis=0, concat_axis=0, tiled=True)  49.1 us
    dot_general x8, matrix products, local(): jnp.einsum('lij,plj->pli', dipole, gathered[:, 1:], precision=highest)  45 us
    dot_general x8, matrix products, local(): jnp.einsum('lji,plj->pli', dipole, inner_part, precision=highest)  31.9 us
    ppermute x8, starting transfers between devices, with_halo(): lax.ppermute(tail, axis, [(i, (i + 1) % count) for i in range(ends)])  28.3 us
    ppermute x8, starting transfers between devices, with_halo(): lax.ppermute(head, axis, [((i + 1) % count, i) for i in range(ends)])  19.2 us
  transfers between devices with their start and end apart: 64, of which 9 were waited for; matrix products, arithmetic and copies ran while one was open for 24% of the time, Pallas kernels for 0%

commit v1 on v0

--- a/solution.py
+++ b/solution.py
@@ -52,7 +52,7 @@
 def broadcast_by_axis(shard, axes, root):
     shard = jnp.where(lax.axis_index(axes) == root, shard, jnp.zeros_like(shard))
     for axis in axes:
-        shard = lax.psum(shard, axis)
+        shard = jnp.sum(lax.all_gather(shard, axis), axis=0)
     return shard
 
 

time: 608 us -> 713 us (1.17)
  blocking collectives: 147 us -> 235 us
  local copies, waits for them, and re-layouts: 38.2 us -> 50.5 us
  starting transfers between devices: 226 us -> 237 us
    all_gather x0 -> x16, blocking collectives: none -> 165 us  [broadcast_by_axis(): shard = jnp.sum(lax.all_gather(shard, axis), axis=0)]
    psum x14 -> x8, blocking collectives: 129 us -> 70.1 us  [one_axis_at_a_time(): return functools.reduce(lax.psum, axes, shard)]
    psum x2 -> x0, blocking collectives: 17.5 us -> none  [broadcast_by_axis(): shard = lax.psum(shard, axis)]
    all_to_all x8, starting transfers between devices: 54.6 us -> 63.3 us  [from_everyone(): return lax.all_to_all(copies, axis, split_axis=0, concat_axis=0, tiled=True)]
    select_n x0 -> x8, local copies, waits for them, and re-layouts: none -> 7.26 us  [broadcast_by_axis(): jnp.where(lax.axis_index(axes) == root, shard, jnp.zeros_like(shard))]
  transfers between devices with their start and end apart: 64 -> 64, of which waited for: 9 -> 9; matrix products, arithmetic and copies ran while one was open for 24% -> 21% of each run, Pallas kernels for 0% -> 0%
where the time goes in v1:
time: 713 us; the launch traced here: 701 us
  starting transfers between devices  237 us (33%)
  blocking collectives  235 us (33%)
  matrix products  114 us (16%)
  local copies, waits for them, and re-layouts  50.5 us (7%)
  other arithmetic  35.5 us (5%)
  waiting for transfers between devices  24.8 us (3%)
    all_gather x16, blocking collectives, broadcast_by_axis(): shard = jnp.sum(lax.all_gather(shard, axis), axis=0)  165 us
    ppermute x32, starting transfers between devices, from_behind(): return lax.ppermute(block, axis, route)  72.5 us
    psum x8, blocking collectives, one_axis_at_a_time(): return functools.reduce(lax.psum, axes, shard)  70.1 us
    all_to_all x8, starting transfers between devices, from_everyone(): return lax.all_to_all(copies, axis, split_axis=0, concat_axis=0, tiled=True)  63.3 us
    all_to_all x8, starting transfers between devices, sum_at_owner(): lax.all_to_all(tiles, axis, split_axis=0, concat_axis=0, tiled=True)  54.5 us
    dot_general x8, matrix products, local(): jnp.einsum('lij,plj->pli', dipole, gathered[:, 1:], precision=highest)  45 us
    dot_general x8, matrix products, local(): jnp.einsum('lji,plj->pli', dipole, inner_part, precision=highest)  32 us
    ppermute x8, starting transfers between devices, with_halo(): lax.ppermute(tail, axis, [(i, (i + 1) % count) for i in range(ends)])  27.3 us
  transfers between devices with their start and end apart: 64, of which 9 were waited for; matrix products, arithmetic and copies ran while one was open for 21% of the time, Pallas kernels for 0%

profile of v1, /device:TPU:88, one launch (start us, length us, event | category | flops | bytes accessed | tf_op | source)
XLA Modules:
  0.0 700.9 jit_solution(13230986992171021854)
XLA Ops:
  9.0 7.2 %all-to-all-start.1 = ((f32[16,2,4,128]{3,1,2,0:T(2,128)}), f32[16,2,4,128]{3,1,2,0:T(2,128)S(1)}, u32[]{:S(2)}, u32[]{:S(2)}) async-start(f32[16,2,4,128]{3,1,2,0:T(2,128)} %bitcast.496), calls=%async_computation.1 | async-start | bytes 131072 | tf_op jit(solution)/shard_map/all_to_all | solution.py:23
  30.4 11.0 %all-gather = f32[8,160,1]{1,2,0:T(1,128)S(1)} all-gather(f32[2,160,1]{1,2,0:T(1,128)S(1)} %copy.65), channel_id=2, replica_groups=mesh['inner'=8,'outer_0'=4,'outer_1'=4] {'outer_0'}, dimensions={0}, use_global_device_ids=true | all-gather | bytes 6400 | tf_op jit(solution)/shard_map/all_gather | solution.py:55
  41.4 10.1 %all-gather.16 = f32[4,2,160]{2,1,0:T(2,128)S(1)} all-gather(f32[1,2,160]{2,1,0:T(2,128)S(1)} %bitcast.534), channel_id=3, replica_groups=mesh['inner'=8,'outer_0'=4,'outer_1'=4] {'outer_1'}, dimensions={0}, use_global_device_ids=true | all-gather | bytes 6400 | tf_op jit(solution)/shard_map/all_gather | solution.py:55
  52.4 8.1 %all-to-all-start = ((f32[16,2,5,128]{3,1,2,0:T(2,128)}), f32[16,2,5,128]{3,1,2,0:T(2,128)S(1)}, u32[]{:S(2)}, u32[]{:S(2)}) async-start(f32[16,2,5,128]{3,1,2,0:T(2,128)} %broadcast_in_dim.156), calls=%async_computation | async-start | bytes 163840 | tf_op jit(solution)/shard_map/all_to_all | solution.py:45
  66.4 5.4 convolution_bitcast_fusion.31
  75.0 8.9 %all-reduce.7 = (f32[2,4,40]{2,0,1:T(2,128)S(1)}, f32[2,4,40]{2,0,1:T(2,128)S(1)}) all-reduce(f32[2,4,40]{2,0,1:T(2,128)S(1)} %convolution_bitcast_fusion.39, f32[2,4,40]{2,0,1:T(2,128)S(1)} %convolution_bitcast_fusion.38), channel_id=1, replica_groups=mesh['inner'=8,'outer_0'=4,'outer_1'=4] {'outer_0'}, use_global_device_ids=true, to_apply=%region_4.5 | all-reduce | flops 640 | bytes 5120 | tf_op jit(solution)/shard_map/psum | solution.py:28
  86.6 5.3 all-to-all-start.3
  91.9 8.0 %all-reduce.3 = (f32[2,160]{1,0:T(2,128)S(1)}, f32[2,160]{1,0:T(2,128)}) all-reduce(f32[2,160]{1,0:T(2,128)S(1)} %mul.604, f32[2,160]{1,0:T(2,128)S(1)} %mul.626), channel_id=1, replica_groups=mesh['inner'=8,'outer_0'=4,'outer_1'=4] {'outer_1'}, use_global_device_ids=true, to_apply=%region_5.6 | all-reduce | flops 640 | bytes 5120 | tf_op jit(solution)/shard_map/psum | solution.py:28
  100.6 8.1 %all-to-all-start.2 = ((f32[16,2,5,128]{3,1,2,0:T(2,128)}), f32[16,2,5,128]{3,1,2,0:T(2,128)S(1)}, u32[]{:S(2)}, u32[]{:S(2)}) async-start(f32[16,2,5,128]{3,1,2,0:T(2,128)} %broadcast_in_dim.159), calls=%async_computation.2 | async-start | bytes 163840 | tf_op jit(solution)/shard_map/all_to_all | solution.py:45
  114.6 5.2 convolution_bitcast_fusion.30
  124.8 10.4 %all-gather.2 = f32[8,160,1]{1,2,0:T(1,128)S(1)} all-gather(f32[2,160,1]{1,2,0:T(1,128)S(1)} %copy.75), channel_id=4, replica_groups=mesh['inner'=8,'outer_0'=4,'outer_1'=4] {'outer_0'}, dimensions={0}, use_global_device_ids=true | all-gather | bytes 6400 | tf_op jit(solution)/shard_map/all_gather | solution.py:55
  135.2 10.1 %all-gather.17 = f32[4,2,160]{2,1,0:T(2,128)S(1)} all-gather(f32[1,2,160]{2,1,0:T(2,128)S(1)} %bitcast.535), channel_id=5, replica_groups=mesh['inner'=8,'outer_0'=4,'outer_1'=4] {'outer_1'}, dimensions={0}, use_global_device_ids=true | all-gather | bytes 6400 | tf_op jit(solution)/shard_map/all_gather | solution.py:55
  161.0 7.8 %all-to-all-start.5 = ((f32[16,2,4,128]{3,1,2,0:T(2,128)}), f32[16,2,4,128]{3,1,2,0:T(2,128)S(1)}, u32[]{:S(2)}, u32[]{:S(2)}) async-start(f32[16,2,4,128]{3,1,2,0:T(2,128)} %bitcast.492), calls=%async_computation.5 | async-start | bytes 131072 | tf_op jit(solution)/shard_map/all_to_all | solution.py:23
  175.3 7.3 %all-to-all-start.4 = ((f32[16,2,5,128]{3,1,2,0:T(2,128)}), f32[16,2,5,128]{3,1,2,0:T(2,128)S(1)}, u32[]{:S(2)}, u32[]{:S(2)}) async-start(f32[16,2,5,128]{3,1,2,0:T(2,128)} %broadcast_in_dim.164), calls=%async_computation.4 | async-start | bytes 163840 | tf_op jit(solution)/shard_map/all_to_all | solution.py:45
  188.4 5.2 convolution_bitcast_fusion.29
  202.4 10.4 %all-gather.4 = f32[8,160,1]{1,2,0:T(1,128)S(1)} all-gather(f32[2,160,1]{1,2,0:T(1,128)S(1)} %copy.82), channel_id=6, replica_groups=mesh['inner'=8,'outer_0'=4,'outer_1'=4] {'outer_0'}, dimensions={0}, use_global_device_ids=true | all-gather | bytes 6400 | tf_op jit(solution)/shard_map/all_gather | solution.py:55
  212.9 10.5 %all-gather.18 = f32[4,2,160]{2,1,0:T(2,128)S(1)} all-gather(f32[1,2,160]{2,1,0:T(2,128)S(1)} %bitcast.536), channel_id=7, replica_groups=mesh['inner'=8,'outer_0'=4,'outer_1'=4] {'outer_1'}, dimensions={0}, use_global_device_ids=true | all-gather | bytes 6400 | tf_op jit(solution)/shard_map/all_gather | solution.py:55
  234.6 8.6 %all-reduce.6 = (f32[2,4,40]{2,0,1:T(2,128)S(1)}, f32[2,4,40]{2,0,1:T(2,128)S(1)}) all-reduce(f32[2,4,40]{2,0,1:T(2,128)S(1)} %convolution_bitcast_fusion.37, f32[2,4,40]{2,0,1:T(2,128)S(1)} %convolution_bitcast_fusion.36), channel_id=1, replica_groups=mesh['inner'=8,'outer_0'=4,'outer_1'=4] {'outer_0'}, use_global_device_ids=true, to_apply=%region_14.15 | all-reduce | flops 640 | bytes 5120 | tf_op jit(solution)/shard_map/psum | solution.py:28
  246.0 6.6 all-to-all-start.7
  258.4 8.4 %all-reduce.2 = (f32[2,160]{1,0:T(2,128)S(1)}, f32[2,160]{1,0:T(2,128)}) all-reduce(f32[2,160]{1,0:T(2,128)S(1)} %mul.648, f32[2,160]{1,0:T(2,128)S(1)} %mul.669), channel_id=1, replica_groups=mesh['inner'=8,'outer_0'=4,'outer_1'=4] {'outer_1'}, use_global_device_ids=true, to_apply=%region_15.16 | all-reduce | flops 640 | bytes 5120 | tf_op jit(solution)/shard_map/psum | solution.py:28
  267.5 8.3 %all-to-all-start.6 = ((f32[16,2,5,128]{3,1,2,0:T(2,128)}), f32[16,2,5,128]{3,1,2,0:T(2,128)S(1)}, u32[]{:S(2)}, u32[]{:S(2)}) async-start(f32[16,2,5,128]{3,1,2,0:T(2,128)} %broadcast_in_dim.169), calls=%async_computation.6 | async-start | bytes 163840 | tf_op jit(solution)/shard_map/all_to_all | solution.py:45
  281.6 5.3 convolution_bitcast_fusion.28
  295.4 10.4 %all-gather.6 = f32[8,160,1]{1,2,0:T(1,128)S(1)} all-gather(f32[2,160,1]{1,2,0:T(1,128)S(1)} %copy.89), channel_id=8, replica_groups=mesh['inner'=8,'outer_0'=4,'outer_1'=4] {'outer_0'}, dimensions={0}, use_global_device_ids=true | all-gather | bytes 6400 | tf_op jit(solution)/shard_map/all_gather | solution.py:55
  305.9 10.1 %all-gather.19 = f32[4,2,160]{2,1,0:T(2,128)S(1)} all-gather(f32[1,2,160]{2,1,0:T(2,128)S(1)} %bitcast.537), channel_id=9, replica_groups=mesh['inner'=8,'outer_0'=4,'outer_1'=4] {'outer_1'}, dimensions={0}, use_global_device_ids=true | all-gather | bytes 6400 | tf_op jit(solution)/shard_map/all_gather | solution.py:55
  331.7 7.8 %all-to-all-start.9 = ((f32[16,2,4,128]{3,1,2,0:T(2,128)}), f32[16,2,4,128]{3,1,2,0:T(2,128)S(1)}, u32[]{:S(2)}, u32[]{:S(2)}) async-start(f32[16,2,4,128]{3,1,2,0:T(2,128)} %bitcast.530), calls=%async_computation.9 | async-start | bytes 131072 | tf_op jit(solution)/shard_map/all_to_all | solution.py:23
  347.2 7.3 %all-to-all-start.8 = ((f32[16,2,5,128]{3,1,2,0:T(2,128)}), f32[16,2,5,128]{3,1,2,0:T(2,128)S(1)}, u32[]{:S(2)}, u32[]{:S(2)}) async-start(f32[16,2,5,128]{3,1,2,0:T(2,128)} %broadcast_in_dim.174), calls=%async_computation.8 | async-start | bytes 163840 | tf_op jit(solution)/shard_map/all_to_all | solution.py:45
  360.4 5.9 convolution_bitcast_fusion.27
  374.0 10.4 %all-gather.8 = f32[8,160,1]{1,2,0:T(1,128)S(1)} all-gather(f32[2,160,1]{1,2,0:T(1,128)S(1)} %copy.96), channel_id=10, replica_groups=mesh['inner'=8,'outer_0'=4,'outer_1'=4] {'outer_0'}, dimensions={0}, use_global_device_ids=true | all-gather | bytes 6400 | tf_op jit(solution)/shard_map/all_gather | solution.py:55
  384.4 10.1 %all-gather.20 = f32[4,2,160]{2,1,0:T(2,128)S(1)} all-gather(f32[1,2,160]{2,1,0:T(2,128)S(1)} %bitcast.538), channel_id=11, replica_groups=mesh['inner'=8,'outer_0'=4,'outer_1'=4] {'outer_1'}, dimensions={0}, use_global_device_ids=true | all-gather | bytes 6400 | tf_op jit(solution)/shard_map/all_gather | solution.py:55
  407.0 9.8 %all-reduce.5 = (f32[2,4,40]{2,0,1:T(2,128)}, f32[2,4,40]{2,0,1:T(2,128)}) all-reduce(f32[2,4,40]{2,0,1:T(2,128)S(1)} %copy-done.80, f32[2,4,40]{2,0,1:T(2,128)S(1)} %convolution_bitcast_fusion.34), channel_id=1, replica_groups=mesh['inner'=8,'outer_0'=4,'outer_1'=4] {'outer_0'}, use_global_device_ids=true, to_apply=%region_24.25 | all-reduce | flops 640 | bytes 5120 | tf_op jit(solution)/shard_map/psum | solution.py:28
  421.5 6.0 all-to-all-start.11
  435.2 8.2 %all-reduce.1 = (f32[2,160]{1,0:T(2,128)}, f32[2,160]{1,0:T(2,128)}) all-reduce(f32[2,160]{1,0:T(2,128)S(1)} %mul.688, f32[2,160]{1,0:T(2,128)} %mul.704), channel_id=1, replica_groups=mesh['inner'=8,'outer_0'=4,'outer_1'=4] {'outer_1'}, use_global_device_ids=true, to_apply=%region_25.26 | all-reduce | flops 640 | bytes 5120 | tf_op jit(solution)/shard_map/psum | solution.py:28
  445.4 8.6 %all-to-all-start.10 = ((f32[16,2,5,128]{3,1,2,0:T(2,128)}), f32[16,2,5,128]{3,1,2,0:T(2,128)S(1)}, u32[]{:S(2)}, u32[]{:S(2)}) async-start(f32[16,2,5,128]{3,1,2,0:T(2,128)} %broadcast_in_dim.179), calls=%async_computation.10 | async-start | bytes 163840 | tf_op jit(solution)/shard_map/all_to_all | solution.py:45
  459.8 5.9 convolution_bitcast_fusion.26
  475.0 10.4 %all-gather.10 = f32[8,160,1]{1,2,0:T(1,128)S(1)} all-gather(f32[2,160,1]{1,2,0:T(1,128)S(1)} %copy.106), channel_id=12, replica_groups=mesh['inner'=8,'outer_0'=4,'outer_1'=4] {'outer_0'}, dimensions={0}, use_global_device_ids=true | all-gather | bytes 6400 | tf_op jit(solution)/shard_map/all_gather | solution.py:55
  485.5 10.1 %all-gather.21 = f32[4,2,160]{2,1,0:T(2,128)S(1)} all-gather(f32[1,2,160]{2,1,0:T(2,128)S(1)} %bitcast.539), channel_id=13, replica_groups=mesh['inner'=8,'outer_0'=4,'outer_1'=4] {'outer_1'}, dimensions={0}, use_global_device_ids=true | all-gather | bytes 6400 | tf_op jit(solution)/shard_map/all_gather | solution.py:55
  511.9 7.8 %all-to-all-start.13 = ((f32[16,2,4,128]{3,1,2,0:T(2,128)}), f32[16,2,4,128]{3,1,2,0:T(2,128)S(1)}, u32[]{:S(2)}, u32[]{:S(2)}) async-start(f32[16,2,4,128]{3,1,2,0:T(2,128)} %bitcast.529), calls=%async_computation.13 | async-start | bytes 131072 | tf_op jit(solution)/shard_map/all_to_all | solution.py:23
  527.4 7.3 %all-to-all-start.12 = ((f32[16,2,5,128]{3,1,2,0:T(2,128)}), f32[16,2,5,128]{3,1,2,0:T(2,128)S(1)}, u32[]{:S(2)}, u32[]{:S(2)}) async-start(f32[16,2,5,128]{3,1,2,0:T(2,128)} %broadcast_in_dim.184), calls=%async_computation.12 | async-start | bytes 163840 | tf_op jit(solution)/shard_map/all_to_all | solution.py:45
  540.5 6.0 convolution_bitcast_fusion.25
  554.9 10.4 %all-gather.12 = f32[8,160,1]{1,2,0:T(1,128)S(1)} all-gather(f32[2,160,1]{1,2,0:T(1,128)S(1)} %copy.113), channel_id=14, replica_groups=mesh['inner'=8,'outer_0'=4,'outer_1'=4] {'outer_0'}, dimensions={0}, use_global_device_ids=true | all-gather | bytes 6400 | tf_op jit(solution)/shard_map/all_gather | solution.py:55
  565.4 10.4 %all-gather.22 = f32[4,2,160]{2,1,0:T(2,128)S(1)} all-gather(f32[1,2,160]{2,1,0:T(2,128)S(1)} %bitcast.540), channel_id=15, replica_groups=mesh['inner'=8,'outer_0'=4,'outer_1'=4] {'outer_1'}, dimensions={0}, use_global_device_ids=true | all-gather | bytes 6400 | tf_op jit(solution)/shard_map/all_gather | solution.py:55
  587.9 9.6 %all-reduce.4 = (f32[2,4,40]{2,0,1:T(2,128)}, f32[2,4,40]{2,0,1:T(2,128)}) all-reduce(f32[2,4,40]{2,0,1:T(2,128)S(1)} %copy-done.79, f32[2,4,40]{2,0,1:T(2,128)S(1)} %convolution_bitcast_fusion.32), channel_id=1, replica_groups=mesh['inner'=8,'outer_0'=4,'outer_1'=4] {'outer_0'}, use_global_device_ids=true, to_apply=%region_34.35 | all-reduce | flops 640 | bytes 5120 | tf_op jit(solution)/shard_map/psum | solution.py:28
  602.2 6.1 all-to-all-start.15
  614.2 8.5 %all-reduce = (f32[2,160]{1,0:T(2,128)}, f32[2,160]{1,0:T(2,128)}) all-reduce(f32[2,160]{1,0:T(2,128)S(1)} %mul.720, f32[2,160]{1,0:T(2,128)} %mul.734), channel_id=1, replica_groups=mesh['inner'=8,'outer_0'=4,'outer_1'=4] {'outer_1'}, use_global_device_ids=true, to_apply=%region_35.36 | all-reduce | flops 640 | bytes 5120 | tf_op jit(solution)/shard_map/psum | solution.py:28
  624.7 8.3 %all-to-all-start.14 = ((f32[16,2,5,128]{3,1,2,0:T(2,128)}), f32[16,2,5,128]{3,1,2,0:T(2,128)S(1)}, u32[]{:S(2)}, u32[]{:S(2)}) async-start(f32[16,2,5,128]{3,1,2,0:T(2,128)} %broadcast_in_dim.189), calls=%async_computation.14 | async-start | bytes 163840 | tf_op jit(solution)/shard_map/all_to_all | solution.py:45
  638.8 6.0 convolution_bitcast_fusion.24
  660.4 10.4 %all-gather.14 = f32[8,160,1]{1,2,0:T(1,128)S(1)} all-gather(f32[2,160,1]{1,2,0:T(1,128)S(1)} %copy.120), channel_id=16, replica_groups=mesh['inner'=8,'outer_0'=4,'outer_1'=4] {'outer_0'}, dimensions={0}, use_global_device_ids=true | all-gather | bytes 6400 | tf_op jit(solution)/shard_map/all_gather | solution.py:55
  670.8 10.1 %all-gather.23 = f32[4,2,160]{2,1,0:T(2,128)S(1)} all-gather(f32[1,2,160]{2,1,0:T(2,128)S(1)} %bitcast.541), channel_id=17, replica_groups=mesh['inner'=8,'outer_0'=4,'outer_1'=4] {'outer_1'}, dimensions={0}, use_global_device_ids=true | all-gather | bytes 6400 | tf_op jit(solution)/shard_map/all_gather | solution.py:55
  (583 shorter events, 299.0 us)
Async XLA Ops:
  2.2 49.5 %collective-permute-start = (f32[2,128]{1,0:T(2,128)S(1)}, f32[2,128]{1,0:T(2,128)S(1)}, u32[]{:S(2)}, u32[]{:S(2)}) collective-permute-start(f32[2,128]{1,0:T(2,128)S(1)} %slice_bitcast_fusion.31), channel_id=1, source_target_pairs={{16,0},{32,16},{48,32},{64,48},{80,64},{96,80},{112,96},{17,1},{33... | collective-permute-start | bytes 3080 | tf_op jit(solution)/shard_map/ppermute | solution.py:34
  9.0 42.7 %all-to-all-start.1 = ((f32[16,2,4,128]{3,1,2,0:T(2,128)}), f32[16,2,4,128]{3,1,2,0:T(2,128)S(1)}, u32[]{:S(2)}, u32[]{:S(2)}) async-start(f32[16,2,4,128]{3,1,2,0:T(2,128)} %bitcast.496), calls=%async_computation.1 | async-start | bytes 131072 | tf_op jit(solution)/shard_map/all_to_all | solution.py:23
  16.2 103.6 %collective-permute-start.6 = (f32[2,40,512]{2,1,0:T(8,128)S(1)}, f32[2,40,512]{2,1,0:T(8,128)S(1)}, u32[]{:S(2)}, u32[]{:S(2)}) collective-permute-start(f32[2,40,512]{2,1,0:T(8,128)S(1)} %slice_bitcast_fusion.15), channel_id=1, source_target_pairs={{16,0},{32,16},{48,32},{64,48},{80,64},{96,80},{112,96},{17,1},{33... | collective-permute-start | bytes 491528 | tf_op jit(solution)/shard_map/ppermute | solution.py:34
  19.0 102.3 %collective-permute-start.4 = (f32[2,160,1]{2,1,0:T(8,128)}, f32[2,160,1]{2,1,0:T(8,128)S(1)}, u32[]{:S(2)}, u32[]{:S(2)}) collective-permute-start(f32[2,160,1]{2,1,0:T(8,128)} %get-tuple-element.61), channel_id=1, source_target_pairs={{0,1},{1,2},{2,3},{3,4},{4,5},{5,6},{6,7},{7,8},{8,9},{9,10},{10,1... | collective-permute-start | bytes 3848 | tf_op jit(solution)/shard_map/ppermute | solution.py:67
  22.3 98.9 %collective-permute-start.5 = (f32[2,160,1]{2,1,0:T(8,128)}, f32[2,160,1]{2,1,0:T(8,128)S(1)}, u32[]{:S(2)}, u32[]{:S(2)}) collective-permute-start(f32[2,160,1]{2,1,0:T(8,128)} %get-tuple-element.63), channel_id=1, source_target_pairs={{1,0},{2,1},{3,2},{4,3},{5,4},{6,5},{7,6},{8,7},{9,8},{10,9},{11,1... | collective-permute-start | bytes 3848 | tf_op jit(solution)/shard_map/ppermute | solution.py:69
  26.3 93.5 %collective-permute-start.7 = (f32[2,40,512]{2,1,0:T(8,128)}, f32[2,40,512]{2,1,0:T(8,128)S(1)}, u32[]{:S(2)}, u32[]{:S(2)}) collective-permute-start(f32[2,40,512]{2,1,0:T(8,128)} %slice_bitcast_fusion.14), channel_id=1, source_target_pairs={{0,16},{16,32},{32,48},{48,64},{64,80},{80,96},{96,112},{1,17},{17... | collective-permute-start | bytes 491528 | tf_op jit(solution)/shard_map/ppermute | solution.py:34
  108.8 36.7 %collective-permute-start.3 = (f32[2,128]{1,0:T(2,128)S(1)}, f32[2,128]{1,0:T(2,128)S(1)}, u32[]{:S(2)}, u32[]{:S(2)}) collective-permute-start(f32[2,128]{1,0:T(2,128)S(1)} %slice_bitcast_fusion.28), channel_id=1, source_target_pairs={{0,16},{16,32},{32,48},{48,64},{64,80},{80,96},{96,112},{1,17},{17... | collective-permute-start | bytes 3080 | tf_op jit(solution)/shard_map/ppermute | solution.py:34
  152.5 22.2 %collective-permute-start.8 = (f32[2,128]{1,0:T(2,128)}, f32[2,128]{1,0:T(2,128)S(1)}, u32[]{:S(2)}, u32[]{:S(2)}) collective-permute-start(f32[2,128]{1,0:T(2,128)} %slice_bitcast_fusion.27), channel_id=1, source_target_pairs={{16,0},{32,16},{48,32},{64,48},{80,64},{96,80},{112,96},{17,1},{33... | collective-permute-start | bytes 3080 | tf_op jit(solution)/shard_map/ppermute | solution.py:34
  154.7 39.0 %collective-permute-start.13 = (f32[2,40,512]{2,1,0:T(8,128)}, f32[2,40,512]{2,1,0:T(8,128)S(1)}, u32[]{:S(2)}, u32[]{:S(2)}) collective-permute-start(f32[2,40,512]{2,1,0:T(8,128)} %slice_bitcast_fusion.12), channel_id=1, source_target_pairs={{0,16},{16,32},{32,48},{48,64},{64,80},{80,96},{96,112},{1,17},{17... | collective-permute-start | bytes 491528 | tf_op jit(solution)/shard_map/ppermute | solution.py:34
  157.2 36.5 %collective-permute-start.12 = (f32[2,40,512]{2,1,0:T(8,128)}, f32[2,40,512]{2,1,0:T(8,128)}, u32[]{:S(2)}, u32[]{:S(2)}) collective-permute-start(f32[2,40,512]{2,1,0:T(8,128)} %slice_bitcast_fusion.13), channel_id=1, source_target_pairs={{16,0},{32,16},{48,32},{64,48},{80,64},{96,80},{112,96},{17,1},{33... | collective-permute-start | bytes 491528 | tf_op jit(solution)/shard_map/ppermute | solution.py:34
  168.8 27.2 %collective-permute-start.10 = (f32[2,160,1]{2,1,0:T(8,128)}, f32[2,160,1]{2,1,0:T(8,128)}, u32[]{:S(2)}, u32[]{:S(2)}) collective-permute-start(f32[2,160,1]{2,1,0:T(8,128)} %get-tuple-element.56), channel_id=1, source_target_pairs={{0,1},{1,2},{2,3},{3,4},{4,5},{5,6},{6,7},{7,8},{8,9},{9,10},{10,1... | collective-permute-start | bytes 3848 | tf_op jit(solution)/shard_map/ppermute | solution.py:67
  172.1 23.9 %collective-permute-start.11 = (f32[2,160,1]{2,1,0:T(8,128)}, f32[2,160,1]{2,1,0:T(8,128)}, u32[]{:S(2)}, u32[]{:S(2)}) collective-permute-start(f32[2,160,1]{2,1,0:T(8,128)} %get-tuple-element.58), channel_id=1, source_target_pairs={{1,0},{2,1},{3,2},{4,3},{5,4},{6,5},{7,6},{8,7},{9,8},{10,9},{11,1... | collective-permute-start | bytes 3848 | tf_op jit(solution)/shard_map/ppermute | solution.py:69
  182.7 40.8 %collective-permute-start.9 = (f32[2,128]{1,0:T(2,128)S(1)}, f32[2,128]{1,0:T(2,128)S(1)}, u32[]{:S(2)}, u32[]{:S(2)}) collective-permute-start(f32[2,128]{1,0:T(2,128)S(1)} %slice_bitcast_fusion.26), channel_id=1, source_target_pairs={{0,16},{16,32},{32,48},{48,64},{64,80},{80,96},{96,112},{1,17},{17... | collective-permute-start | bytes 3080 | tf_op jit(solution)/shard_map/ppermute | solution.py:34
  228.9 58.1 %collective-permute-start.19 = (f32[2,40,512]{2,1,0:T(8,128)}, f32[2,40,512]{2,1,0:T(8,128)}, u32[]{:S(2)}, u32[]{:S(2)}) collective-permute-start(f32[2,40,512]{2,1,0:T(8,128)} %slice_bitcast_fusion.10), channel_id=1, source_target_pairs={{0,16},{16,32},{32,48},{48,64},{64,80},{80,96},{96,112},{1,17},{17... | collective-permute-start | bytes 491528 | tf_op jit(solution)/shard_map/ppermute | solution.py:34
  230.8 56.1 %collective-permute-start.18 = (f32[2,40,512]{2,1,0:T(8,128)}, f32[2,40,512]{2,1,0:T(8,128)}, u32[]{:S(2)}, u32[]{:S(2)}) collective-permute-start(f32[2,40,512]{2,1,0:T(8,128)} %slice_bitcast_fusion.11), channel_id=1, source_target_pairs={{16,0},{32,16},{48,32},{64,48},{80,64},{96,80},{112,96},{17,1},{33... | collective-permute-start | bytes 491528 | tf_op jit(solution)/shard_map/ppermute | solution.py:34
  243.4 23.4 %collective-permute-start.14 = (f32[2,128]{1,0:T(2,128)S(1)}, f32[2,128]{1,0:T(2,128)S(1)}, u32[]{:S(2)}, u32[]{:S(2)}) collective-permute-start(f32[2,128]{1,0:T(2,128)S(1)} %slice_bitcast_fusion.25), channel_id=1, source_target_pairs={{16,0},{32,16},{48,32},{64,48},{80,64},{96,80},{112,96},{17,1},{33... | collective-permute-start | bytes 3080 | tf_op jit(solution)/shard_map/ppermute | solution.py:34
  246.0 20.8 %all-to-all-start.7 = ((f32[16,2,4,128]{3,1,2,0:T(2,128)}), f32[16,2,4,128]{3,1,2,0:T(2,128)S(1)}, u32[]{:S(2)}, u32[]{:S(2)}) async-start(f32[16,2,4,128]{3,1,2,0:T(2,128)} %bitcast.490), calls=%async_computation.7 | async-start | bytes 131072 | tf_op jit(solution)/shard_map/all_to_all | solution.py:23
  252.6 36.8 %collective-permute-start.16 = (f32[2,160,1]{2,1,0:T(8,128)}, f32[2,160,1]{2,1,0:T(8,128)}, u32[]{:S(2)}, u32[]{:S(2)}) collective-permute-start(f32[2,160,1]{2,1,0:T(8,128)} %get-tuple-element.51), channel_id=1, source_target_pairs={{0,1},{1,2},{2,3},{3,4},{4,5},{5,6},{6,7},{7,8},{8,9},{9,10},{10,1... | collective-permute-start | bytes 3848 | tf_op jit(solution)/shard_map/ppermute | solution.py:67
  255.9 33.4 %collective-permute-start.17 = (f32[2,160,1]{2,1,0:T(8,128)}, f32[2,160,1]{2,1,0:T(8,128)}, u32[]{:S(2)}, u32[]{:S(2)}) collective-permute-start(f32[2,160,1]{2,1,0:T(8,128)} %get-tuple-element.53), channel_id=1, source_target_pairs={{1,0},{2,1},{3,2},{4,3},{5,4},{6,5},{7,6},{8,7},{9,8},{10,9},{11,1... | collective-permute-start | bytes 3848 | tf_op jit(solution)/shard_map/ppermute | solution.py:69
  275.9 40.2 %collective-permute-start.15 = (f32[2,128]{1,0:T(2,128)S(1)}, f32[2,128]{1,0:T(2,128)S(1)}, u32[]{:S(2)}, u32[]{:S(2)}) collective-permute-start(f32[2,128]{1,0:T(2,128)S(1)} %slice_bitcast_fusion.24), channel_id=1, source_target_pairs={{0,16},{16,32},{32,48},{48,64},{64,80},{80,96},{96,112},{1,17},{17... | collective-permute-start | bytes 3080 | tf_op jit(solution)/shard_map/ppermute | solution.py:34
  322.7 22.6 %collective-permute-start.20 = (f32[2,128]{1,0:T(2,128)S(1)}, f32[2,128]{1,0:T(2,128)S(1)}, u32[]{:S(2)}, u32[]{:S(2)}) collective-permute-start(f32[2,128]{1,0:T(2,128)S(1)} %slice_bitcast_fusion.23), channel_id=1, source_target_pairs={{16,0},{32,16},{48,32},{64,48},{80,64},{96,80},{112,96},{17,1},{33... | collective-permute-start | bytes 3080 | tf_op jit(solution)/shard_map/ppermute | solution.py:34
  325.5 40.9 %collective-permute-start.25 = (f32[2,40,512]{2,1,0:T(8,128)}, f32[2,40,512]{2,1,0:T(8,128)}, u32[]{:S(2)}, u32[]{:S(2)}) collective-permute-start(f32[2,40,512]{2,1,0:T(8,128)} %slice_bitcast_fusion.8), channel_id=1, source_target_pairs={{0,16},{16,32},{32,48},{48,64},{64,80},{80,96},{96,112},{1,17},{17... | collective-permute-start | bytes 491528 | tf_op jit(solution)/shard_map/ppermute | solution.py:34
  327.9 38.5 %collective-permute-start.24 = (f32[2,40,512]{2,1,0:T(8,128)}, f32[2,40,512]{2,1,0:T(8,128)}, u32[]{:S(2)}, u32[]{:S(2)}) collective-permute-start(f32[2,40,512]{2,1,0:T(8,128)} %slice_bitcast_fusion.9), channel_id=1, source_target_pairs={{16,0},{32,16},{48,32},{64,48},{80,64},{96,80},{112,96},{17,1},{33... | collective-permute-start | bytes 491528 | tf_op jit(solution)/shard_map/ppermute | solution.py:34
  339.5 29.3 %collective-permute-start.22 = (f32[2,160,1]{2,1,0:T(8,128)}, f32[2,160,1]{2,1,0:T(8,128)}, u32[]{:S(2)}, u32[]{:S(2)}) collective-permute-start(f32[2,160,1]{2,1,0:T(8,128)} %get-tuple-element.46), channel_id=1, source_target_pairs={{0,1},{1,2},{2,3},{3,4},{4,5},{5,6},{6,7},{7,8},{8,9},{9,10},{10,1... | collective-permute-start | bytes 3848 | tf_op jit(solution)/shard_map/ppermute | solution.py:67
  342.8 25.9 %collective-permute-start.23 = (f32[2,160,1]{2,1,0:T(8,128)}, f32[2,160,1]{2,1,0:T(8,128)}, u32[]{:S(2)}, u32[]{:S(2)}) collective-permute-start(f32[2,160,1]{2,1,0:T(8,128)} %get-tuple-element.48), channel_id=1, source_target_pairs={{1,0},{2,1},{3,2},{4,3},{5,4},{6,5},{7,6},{8,7},{9,8},{10,9},{11,1... | collective-permute-start | bytes 3848 | tf_op jit(solution)/shard_map/ppermute | solution.py:69
  357.3 38.2 %collective-permute-start.21 = (f32[2,128]{1,0:T(2,128)}, f32[2,128]{1,0:T(2,128)}, u32[]{:S(2)}, u32[]{:S(2)}) collective-permute-start(f32[2,128]{1,0:T(2,128)} %slice_bitcast_fusion.22), channel_id=1, source_target_pairs={{0,16},{16,32},{32,48},{48,64},{64,80},{80,96},{96,112},{1,17},{17... | collective-permute-start | bytes 3080 | tf_op jit(solution)/shard_map/ppermute | solution.py:34
  403.7 62.1 %collective-permute-start.30 = (f32[2,40,512]{2,1,0:T(8,128)}, f32[2,40,512]{2,1,0:T(8,128)}, u32[]{:S(2)}, u32[]{:S(2)}) collective-permute-start(f32[2,40,512]{2,1,0:T(8,128)} %slice_bitcast_fusion.7), channel_id=1, source_target_pairs={{16,0},{32,16},{48,32},{64,48},{80,64},{96,80},{112,96},{17,1},{33... | collective-permute-start | bytes 491528 | tf_op jit(solution)/shard_map/ppermute | solution.py:34
  418.9 24.5 %collective-permute-start.26 = (f32[2,128]{1,0:T(2,128)}, f32[2,128]{1,0:T(2,128)S(1)}, u32[]{:S(2)}, u32[]{:S(2)}) collective-permute-start(f32[2,128]{1,0:T(2,128)} %slice_bitcast_fusion.21), channel_id=1, source_target_pairs={{16,0},{32,16},{48,32},{64,48},{80,64},{96,80},{112,96},{17,1},{33... | collective-permute-start | bytes 3080 | tf_op jit(solution)/shard_map/ppermute | solution.py:34
  421.5 23.2 %all-to-all-start.11 = ((f32[16,2,4,128]{3,1,2,0:T(2,128)}), f32[16,2,4,128]{3,1,2,0:T(2,128)S(1)}, u32[]{:S(2)}, u32[]{:S(2)}) async-start(f32[16,2,4,128]{3,1,2,0:T(2,128)} %bitcast.527), calls=%async_computation.11 | async-start | bytes 131072 | tf_op jit(solution)/shard_map/all_to_all | solution.py:23
  427.5 40.7 %collective-permute-start.28 = (f32[2,160,1]{2,1,0:T(8,128)}, f32[2,160,1]{2,1,0:T(8,128)}, u32[]{:S(2)}, u32[]{:S(2)}) collective-permute-start(f32[2,160,1]{2,1,0:T(8,128)} %get-tuple-element.41), channel_id=1, source_target_pairs={{0,1},{1,2},{2,3},{3,4},{4,5},{5,6},{6,7},{7,8},{8,9},{9,10},{10,1... | collective-permute-start | bytes 3848 | tf_op jit(solution)/shard_map/ppermute | solution.py:67
  430.8 37.3 %collective-permute-start.29 = (f32[2,160,1]{2,1,0:T(8,128)}, f32[2,160,1]{2,1,0:T(8,128)}, u32[]{:S(2)}, u32[]{:S(2)}) collective-permute-start(f32[2,160,1]{2,1,0:T(8,128)} %get-tuple-element.43), channel_id=1, source_target_pairs={{1,0},{2,1},{3,2},{4,3},{5,4},{6,5},{7,6},{8,7},{9,8},{10,9},{11,1... | collective-permute-start | bytes 3848 | tf_op jit(solution)/shard_map/ppermute | solution.py:69
  433.3 32.5 %collective-permute-start.31 = (f32[2,40,512]{2,1,0:T(8,128)}, f32[2,40,512]{2,1,0:T(8,128)}, u32[]{:S(2)}, u32[]{:S(2)}) collective-permute-start(f32[2,40,512]{2,1,0:T(8,128)} %slice_bitcast_fusion.6), channel_id=1, source_target_pairs={{0,16},{16,32},{32,48},{48,64},{64,80},{80,96},{96,112},{1,17},{17... | collective-permute-start | bytes 491528 | tf_op jit(solution)/shard_map/ppermute | solution.py:34
  456.7 39.0 %collective-permute-start.27 = (f32[2,128]{1,0:T(2,128)}, f32[2,128]{1,0:T(2,128)}, u32[]{:S(2)}, u32[]{:S(2)}) collective-permute-start(f32[2,128]{1,0:T(2,128)} %slice_bitcast_fusion.20), channel_id=1, source_target_pairs={{0,16},{16,32},{32,48},{48,64},{64,80},{80,96},{96,112},{1,17},{17... | collective-permute-start | bytes 3080 | tf_op jit(solution)/shard_map/ppermute | solution.py:34
  502.9 22.6 %collective-permute-start.32 = (f32[2,128]{1,0:T(2,128)S(1)}, f32[2,128]{1,0:T(2,128)S(1)}, u32[]{:S(2)}, u32[]{:S(2)}) collective-permute-start(f32[2,128]{1,0:T(2,128)S(1)} %slice_bitcast_fusion.19), channel_id=1, source_target_pairs={{16,0},{32,16},{48,32},{64,48},{80,64},{96,80},{112,96},{17,1},{33... | collective-permute-start | bytes 3080 | tf_op jit(solution)/shard_map/ppermute | solution.py:34
  505.7 40.9 %collective-permute-start.37 = (f32[2,40,512]{2,1,0:T(8,128)}, f32[2,40,512]{2,1,0:T(8,128)}, u32[]{:S(2)}, u32[]{:S(2)}) collective-permute-start(f32[2,40,512]{2,1,0:T(8,128)} %slice_bitcast_fusion.4), channel_id=1, source_target_pairs={{0,16},{16,32},{32,48},{48,64},{64,80},{80,96},{96,112},{1,17},{17... | collective-permute-start | bytes 491528 | tf_op jit(solution)/shard_map/ppermute | solution.py:34
  508.1 38.5 %collective-permute-start.36 = (f32[2,40,512]{2,1,0:T(8,128)}, f32[2,40,512]{2,1,0:T(8,128)}, u32[]{:S(2)}, u32[]{:S(2)}) collective-permute-start(f32[2,40,512]{2,1,0:T(8,128)} %slice_bitcast_fusion.5), channel_id=1, source_target_pairs={{16,0},{32,16},{48,32},{64,48},{80,64},{96,80},{112,96},{17,1},{33... | collective-permute-start | bytes 491528 | tf_op jit(solution)/shard_map/ppermute | solution.py:34
  519.6 29.2 %collective-permute-start.34 = (f32[2,160,1]{2,1,0:T(8,128)}, f32[2,160,1]{2,1,0:T(8,128)}, u32[]{:S(2)}, u32[]{:S(2)}) collective-permute-start(f32[2,160,1]{2,1,0:T(8,128)} %get-tuple-element.36), channel_id=1, source_target_pairs={{0,1},{1,2},{2,3},{3,4},{4,5},{5,6},{6,7},{7,8},{8,9},{9,10},{10,1... | collective-permute-start | bytes 3848 | tf_op jit(solution)/shard_map/ppermute | solution.py:67
  523.0 25.8 %collective-permute-start.35 = (f32[2,160,1]{2,1,0:T(8,128)}, f32[2,160,1]{2,1,0:T(8,128)}, u32[]{:S(2)}, u32[]{:S(2)}) collective-permute-start(f32[2,160,1]{2,1,0:T(8,128)} %get-tuple-element.38), channel_id=1, source_target_pairs={{1,0},{2,1},{3,2},{4,3},{5,4},{6,5},{7,6},{8,7},{9,8},{10,9},{11,1... | collective-permute-start | bytes 3848 | tf_op jit(solution)/shard_map/ppermute | solution.py:69
  537.4 38.4 %collective-permute-start.33 = (f32[2,128]{1,0:T(2,128)}, f32[2,128]{1,0:T(2,128)}, u32[]{:S(2)}, u32[]{:S(2)}) collective-permute-start(f32[2,128]{1,0:T(2,128)} %slice_bitcast_fusion.18), channel_id=1, source_target_pairs={{0,16},{16,32},{32,48},{48,64},{64,80},{80,96},{96,112},{1,17},{17... | collective-permute-start | bytes 3080 | tf_op jit(solution)/shard_map/ppermute | solution.py:34
  581.8 63.0 %collective-permute-start.43 = (f32[2,40,512]{2,1,0:T(8,128)}, f32[2,40,512]{2,1,0:T(8,128)}, u32[]{:S(2)}, u32[]{:S(2)}) collective-permute-start(f32[2,40,512]{2,1,0:T(8,128)} %slice_bitcast_fusion.2), channel_id=1, source_target_pairs={{0,16},{16,32},{32,48},{48,64},{64,80},{80,96},{96,112},{1,17},{17... | collective-permute-start | bytes 491528 | tf_op jit(solution)/shard_map/ppermute | solution.py:34
  583.8 61.1 %collective-permute-start.42 = (f32[2,40,512]{2,1,0:T(8,128)}, f32[2,40,512]{2,1,0:T(8,128)}, u32[]{:S(2)}, u32[]{:S(2)}) collective-permute-start(f32[2,40,512]{2,1,0:T(8,128)} %slice_bitcast_fusion.3), channel_id=1, source_target_pairs={{16,0},{32,16},{48,32},{64,48},{80,64},{96,80},{112,96},{17,1},{33... | collective-permute-start | bytes 491528 | tf_op jit(solution)/shard_map/ppermute | solution.py:34
  599.6 23.1 %collective-permute-start.38 = (f32[2,128]{1,0:T(2,128)}, f32[2,128]{1,0:T(2,128)S(1)}, u32[]{:S(2)}, u32[]{:S(2)}) collective-permute-start(f32[2,128]{1,0:T(2,128)} %slice_bitcast_fusion.17), channel_id=1, source_target_pairs={{16,0},{32,16},{48,32},{64,48},{80,64},{96,80},{112,96},{17,1},{33... | collective-permute-start | bytes 3080 | tf_op jit(solution)/shard_map/ppermute | solution.py:34
  602.2 21.8 %all-to-all-start.15 = ((f32[16,2,4,128]{3,1,2,0:T(2,128)}), f32[16,2,4,128]{3,1,2,0:T(2,128)S(1)}, u32[]{:S(2)}, u32[]{:S(2)}) async-start(f32[16,2,4,128]{3,1,2,0:T(2,128)} %bitcast.528), calls=%async_computation.15 | async-start | bytes 131072 | tf_op jit(solution)/shard_map/all_to_all | solution.py:23
  608.3 38.8 %collective-permute-start.40 = (f32[2,160,1]{2,1,0:T(8,128)}, f32[2,160,1]{2,1,0:T(8,128)}, u32[]{:S(2)}, u32[]{:S(2)}) collective-permute-start(f32[2,160,1]{2,1,0:T(8,128)} %get-tuple-element.31), channel_id=1, source_target_pairs={{0,1},{1,2},{2,3},{3,4},{4,5},{5,6},{6,7},{7,8},{8,9},{9,10},{10,1... | collective-permute-start | bytes 3848 | tf_op jit(solution)/shard_map/ppermute | solution.py:67
  611.7 35.5 %collective-permute-start.41 = (f32[2,160,1]{2,1,0:T(8,128)}, f32[2,160,1]{2,1,0:T(8,128)}, u32[]{:S(2)}, u32[]{:S(2)}) collective-permute-start(f32[2,160,1]{2,1,0:T(8,128)} %get-tuple-element.33), channel_id=1, source_target_pairs={{1,0},{2,1},{3,2},{4,3},{5,4},{6,5},{7,6},{8,7},{9,8},{10,9},{11,1... | collective-permute-start | bytes 3848 | tf_op jit(solution)/shard_map/ppermute | solution.py:69
  635.6 45.5 %collective-permute-start.39 = (f32[2,128]{1,0:T(2,128)}, f32[2,128]{1,0:T(2,128)}, u32[]{:S(2)}, u32[]{:S(2)}) collective-permute-start(f32[2,128]{1,0:T(2,128)} %slice_bitcast_fusion.16), channel_id=1, source_target_pairs={{0,16},{16,32},{32,48},{48,64},{64,80},{80,96},{96,112},{1,17},{17... | collective-permute-start | bytes 3080 | tf_op jit(solution)/shard_map/ppermute | solution.py:34
  652.9 36.3 %collective-permute-start.47 = (f32[2,40,512]{2,1,0:T(8,128)}, f32[2,40,512]{2,1,0:T(8,128)}, u32[]{:S(2)}, u32[]{:S(2)}) collective-permute-start(f32[2,40,512]{2,1,0:T(8,128)} %slice_bitcast_fusion), channel_id=1, source_target_pairs={{0,16},{16,32},{32,48},{48,64},{64,80},{80,96},{96,112},{1,17},{17... | collective-permute-start | bytes 491528 | tf_op jit(solution)/shard_map/ppermute | solution.py:34
  655.4 33.9 %collective-permute-start.46 = (f32[2,40,512]{2,1,0:T(8,128)}, f32[2,40,512]{2,1,0:T(8,128)}, u32[]{:S(2)}, u32[]{:S(2)}) collective-permute-start(f32[2,40,512]{2,1,0:T(8,128)} %slice_bitcast_fusion.1), channel_id=1, source_target_pairs={{16,0},{32,16},{48,32},{64,48},{80,64},{96,80},{112,96},{17,1},{33... | collective-permute-start | bytes 491528 | tf_op jit(solution)/shard_map/ppermute | solution.py:34
  (128 other events, 3123.6 us)
